TPU v7x, 128 devices: a whole 4x4x4 slice. The times are simulated.
128 devices in a mesh: grp: 8 (over y, core), dev: 16 (over x, z).
Axes of the slice: x: 4, y: 4, z: 4, core: 2. Of those that a mesh axis runs over, the one named last changes fastest.
Arguments:
- tiles: bfloat16 [65536, 128, 128], P(('grp', 'dev')), may hold values from -0.125 to 0.125
- tile_ray: int32 [65536], P(('grp', 'dev')), may hold values from 0 to 31, as said below
- tile_col: int32 [65536], P(('grp', 'dev')), may hold values from 0 to 23, as said below
- touched: int32 [3072], P(('grp', 'dev')), may hold values from 0 to 8191, as said below
- home: int32 [8192], replicated, may hold values from 0 to 8191, as said below
- sketch: bfloat16 [1048576, 128], P(('grp', 'dev')), may hold values from -6 to 6
Outputs:
- basis: float32 [1048576, 128], P(('grp', 'dev'))
- r_factor: float32 [128, 128], replicated
Inputs may be any that keep to these rules, and one draw needn't show every extreme that they name: `home`: A permutation that maps each region of 1024 consecutive voxel blocks, g * 1024 to (g + 1) * 1024 - 1, onto the same range of positions. The 24 entries of device i along grp+dev are distinct voxel blocks whose positions home[v] lie in the region of its group g = i // 16; at most 3 of them have positions stored on any one device (position // 64), and in every group one device stores 3 of the touched blocks of every device of the group. On each device the pairs (tile_ray, tile_col) are distinct. `tile_col`: indexes the device's own 24 entries of touched.
All inputs are finite; a program needn't handle non-finite values.
Results may differ from a plain program's by a relative error of at most 0.0017.
Values may be sent and summed in bfloat16 or wider, within the bound.
A program may use at most 192 MiB of HBM per device.

v0:
```python
import jax
import jax.numpy as jnp
from jax import lax
from jax.sharding import PartitionSpec as P

CAP = 3
RB_DEV = 32


gram_shift = 0.001


def factor_lower(gram_matrix):
    width = gram_matrix.shape[0]
    indices = jnp.arange(width, dtype=jnp.int32)

    def column_step(column, lower):
        pick = (indices == column).astype(jnp.float32)
        row_part = jnp.dot(pick, lower, precision=lax.Precision.HIGHEST)
        target = jnp.dot(gram_matrix, pick, precision=lax.Precision.HIGHEST)
        rest = target - jnp.dot(lower, row_part, precision=lax.Precision.HIGHEST)
        diagonal = jnp.sqrt(jnp.sum(rest * pick))
        fresh = jnp.where(
            indices > column, rest / diagonal, jnp.where(indices == column, diagonal, 0.0)
        )
        return lower + fresh[:, None] * pick[None, :]

    return lax.fori_loop(0, width, column_step, jnp.zeros((width, width), jnp.float32))


def invert_lower(lower):
    width = lower.shape[0]
    indices = jnp.arange(width, dtype=jnp.int32)

    def row_step(row, inverse):
        pick = (indices == row).astype(jnp.float32)
        row_part = jnp.dot(pick, lower, precision=lax.Precision.HIGHEST)
        diagonal = jnp.sum(row_part * pick)
        fresh = (pick - jnp.dot(row_part, inverse, precision=lax.Precision.HIGHEST)) / diagonal
        return inverse + pick[:, None] * fresh[None, :]

    return lax.fori_loop(0, width, row_step, jnp.zeros((width, width), jnp.float32))


def local(tiles, tile_ray, tile_col, touched, home, sketch):
    group_size = lax.axis_size("dev")
    tile_size = tiles.shape[1]
    width = sketch.shape[1]
    block_count = sketch.shape[0] // tile_size
    ntouch = touched.shape[0]
    slot_count = group_size * CAP
    matches = touched[:, None] == jnp.arange(home.shape[0], dtype=jnp.int32)[None, :]
    stored = jnp.sum(jnp.where(matches, home[None, :], 0), axis=1)
    holder = stored // block_count % group_size
    local_row = stored % block_count
    counter = jnp.arange(ntouch, dtype=jnp.int32)
    earlier = (holder[:, None] == holder[None, :]) & (counter[:, None] > counter[None, :])
    position = holder * CAP + jnp.sum(earlier, axis=1)
    placing = position[:, None] == jnp.arange(slot_count, dtype=jnp.int32)[None, :]
    request = (jnp.sum(jnp.where(placing, local_row[:, None] + 1, 0), axis=0) - 1).reshape(
        group_size, CAP
    )
    incoming = lax.all_to_all(request, "dev", split_axis=0, concat_axis=0, tiled=True)
    region_block = stored % (group_size * block_count)
    wanted = region_block[:, None] * tile_size + jnp.arange(tile_size, dtype=jnp.int32)[None, :]
    blank_rows = jnp.zeros((ntouch, tile_size, width), sketch.dtype)
    shard_rows = lax.all_gather(sketch, "dev", axis=0, tiled=True)
    length = shard_rows.shape[0]
    inside = (wanted >= 0) & (wanted < length)
    picked = jnp.take(shard_rows, jnp.clip(wanted, 0, length - 1).reshape(-1), axis=0).reshape(
        ntouch, tile_size, width
    )
    touched_rows = jnp.where(inside[:, :, None], picked, blank_rows)
    batch_rows = min(128, tiles.shape[0])
    rounds = tiles.shape[0] // batch_rows
    tile_steps = tiles.reshape(rounds, batch_rows, tile_size, tile_size)
    ray_steps = tile_ray.reshape(rounds, batch_rows)
    col_steps = tile_col.reshape(rounds, batch_rows)

    def image_step(running, inputs):
        tile_block, ray_block, col_block = inputs
        gathered = jnp.take(touched_rows, col_block, axis=0)
        product = jnp.einsum(
            "tab,tbk->tak", tile_block, gathered, preferred_element_type=jnp.float32
        )
        return (running.at[ray_block].add(product), None)

    images, _ = lax.scan(
        image_step,
        jnp.zeros((RB_DEV, tile_size, width), jnp.float32),
        (tile_steps, ray_steps, col_steps),
    )
    images = images.astype(jnp.bfloat16)

    def normal_step(running, inputs):
        tile_block, ray_block, col_block = inputs
        gathered = jnp.take(images, ray_block, axis=0)
        product = jnp.einsum(
            "tab,tak->tbk", tile_block, gathered, preferred_element_type=jnp.float32
        )
        return (running.at[col_block].add(product), None)

    partial_value, _ = lax.scan(
        normal_step,
        jnp.zeros((ntouch, tile_size, width), jnp.float32),
        (tile_steps, ray_steps, col_steps),
    )
    slot_of = jnp.sum(
        jnp.where(placing, jnp.arange(slot_count, dtype=jnp.int32)[None, :], 0), axis=1
    )
    outgoing = jnp.zeros((slot_count, tile_size, width), jnp.float32).at[slot_of].set(partial_value)
    arrived = lax.all_to_all(
        outgoing.reshape(group_size, CAP, tile_size, width),
        "dev",
        split_axis=0,
        concat_axis=0,
        tiled=True,
    )
    target = incoming.reshape(-1)
    safe_target = jnp.where(target >= 0, target, block_count)
    normal = (
        jnp.zeros((block_count + 1, tile_size, width), jnp.float32)
        .at[safe_target]
        .add(arrived.reshape(slot_count, tile_size, width))
    )
    normal = normal[:block_count].reshape(block_count * tile_size, width)
    gram_matrix = lax.psum(
        jnp.dot(normal.T, normal, precision=lax.Precision.HIGHEST), ("grp", "dev")
    )
    voxels = normal.shape[0] * lax.axis_size("grp") * group_size
    gram_matrix = gram_matrix / voxels + gram_shift * jnp.eye(width, dtype=jnp.float32)
    lower = factor_lower(gram_matrix)
    r_factor = lower.T
    inverse = invert_lower(lower).T
    basis_out = jnp.dot(normal, inverse, precision=lax.Precision.HIGHEST)
    return (basis_out, r_factor)


def solution(mesh):
    in_specs = (
        P(("grp", "dev"), None, None),
        P(("grp", "dev")),
        P(("grp", "dev")),
        P(("grp", "dev")),
        P(),
        P(("grp", "dev"), None),
    )
    out_specs = (P(("grp", "dev"), None), P())
    return jax.shard_map(local, mesh=mesh, in_specs=in_specs, out_specs=out_specs, check_vma=False)
```

profile of v0, /device:TPU:1, one launch (start us, length us, event | category | flops | bytes accessed | tf_op | source)
XLA Modules:
  0.0 1192.9 jit_solution(2345552403613061761)
XLA Ops:
  10.0 8.5 all-to-all-start
  18.5 21.4 %copy.22 = bf16[512,128,128]{1,2,0:T(8,128)(2,1)} copy(bf16[512,128,128]{2,1,0:T(8,128)(2,1)} %param.14) | data formatting | bytes 33554432 | tf_op args[0]
  40.1 170.2 %all-gather.2.cloned.1.call-done = bf16[131072,128]{1,0:T(8,128)(2,1)} async-done(((bf16[8192,128]{1,0:T(8,128)(2,1)}), bf16[131072,128]{1,0:T(8,128)(2,1)}) %all-gather.2.cloned.1.call-update) | async-done | bytes 33554448 | tf_op jit(solution)/shard_map/all_gather | solution.py:67
  210.3 32.7 %gather_fusion.2 = bf16[3072,128]{1,0:T(8,128)(2,1)S(1)} fusion(bf16[131072,128]{1,0:T(8,128)(2,1)} %all-gather.2.cloned.1.call-done, s32[3072]{0:T(1024)S(1)} %broadcast_clamp_fusion), kind=kCustom, calls=%fused_computation.2 | custom fusion | bytes 1585152 | tf_op jit(solution)/shard_map/jit(_take)/gather | solution.py:70
  244.4 113.0 %while.49 = (s32[]{:T(128)}, f32[32,128,128]{2,1,0:T(8,128)S(1)}, s32[4,128]{1,0:T(4,128)S(1)}, bf16[4,128,128,128]{3,2,1,0:T(8,128)(2,1)}, s32[4,128]{1,0:T(4,1...) while((s32[]{:T(128)}, f32[32,128,128]{2,1,0:T(8,128)S(1)}, s32[4,128]{1,0:T(4,128)S(1)}, ...), condition=%wide.region_6.7_spmd, body=%wide.region_4.6_spmd.sunk | while | flops 541067776 | bytes 50340692 | solution.py:88
  247.6 8.0 fusion.97
  255.6 17.1 %scatter_fusion = f32[32,128,128]{2,1,0:T(8,128)S(1)} fusion(f32[32,128,128]{2,1,0:T(8,128)S(1)} %get-tuple-element.482, s32[128]{0:T(128)S(1)} %get-tuple-element.454, f32[128,128,128]{2,1,0:T(8,128)} %fusion.97), kind=kCustom, calls=%fused_computation.3.clone.1 | custom fusion | flops 2097152 | bytes 25166336 | tf_op jit(solution)/shard_map/while/body/eval_jaxpr/scatter-add | solution.py:86
  283.9 17.1 %scatter_fusion = f32[32,128,128]{2,1,0:T(8,128)S(1)} fusion(f32[32,128,128]{2,1,0:T(8,128)S(1)} %get-tuple-element.482, s32[128]{0:T(128)S(1)} %get-tuple-element.454, f32[128,128,128]{2,1,0:T(8,128)} %fusion.97), kind=kCustom, calls=%fused_computation.3.clone.1 | custom fusion | flops 2097152 | bytes 25166336 | tf_op jit(solution)/shard_map/while/body/eval_jaxpr/scatter-add | solution.py:86
  304.1 8.0 fusion.97
  312.1 17.1 %scatter_fusion = f32[32,128,128]{2,1,0:T(8,128)S(1)} fusion(f32[32,128,128]{2,1,0:T(8,128)S(1)} %get-tuple-element.482, s32[128]{0:T(128)S(1)} %get-tuple-element.454, f32[128,128,128]{2,1,0:T(8,128)} %fusion.97), kind=kCustom, calls=%fused_computation.3.clone.1 | custom fusion | flops 2097152 | bytes 25166336 | tf_op jit(solution)/shard_map/while/body/eval_jaxpr/scatter-add | solution.py:86
  340.3 17.1 %scatter_fusion = f32[32,128,128]{2,1,0:T(8,128)S(1)} fusion(f32[32,128,128]{2,1,0:T(8,128)S(1)} %get-tuple-element.482, s32[128]{0:T(128)S(1)} %get-tuple-element.454, f32[128,128,128]{2,1,0:T(8,128)} %fusion.97), kind=kCustom, calls=%fused_computation.3.clone.1 | custom fusion | flops 2097152 | bytes 25166336 | tf_op jit(solution)/shard_map/while/body/eval_jaxpr/scatter-add | solution.py:86
  357.7 112.9 %while.50 = (s32[]{:T(128)}, f32[24,128,128]{2,1,0:T(8,128)S(1)}, s32[4,128]{1,0:T(4,128)S(1)}, bf16[4,128,128,128]{2,3,1,0:T(8,128)(2,1)}, s32[4,128]{1,0:T(4,1...) while((s32[]{:T(128)}, f32[24,128,128]{2,1,0:T(8,128)S(1)}, s32[4,128]{1,0:T(4,128)S(1)}, ...), condition=%wide.region_9.10_spmd, body=%wide.region_7.9_spmd.sunk | while | flops 541067776 | bytes 50340692 | solution.py:103
  360.9 8.0 fusion.101
  368.9 17.0 %scatter_fusion.1 = f32[24,128,128]{2,1,0:T(8,128)S(1)} fusion(f32[24,128,128]{2,1,0:T(8,128)S(1)} %get-tuple-element.503, s32[128]{0:T(128)S(1)} %get-tuple-element.462, f32[128,128,128]{2,1,0:T(8,128)} %fusion.101), kind=kCustom, calls=%fused_computation.4.clone.1 | custom fusion | flops 2097152 | bytes 25166336 | tf_op jit(solution)/shard_map/while/body/eval_jaxpr/scatter-add | solution.py:101
  397.2 17.0 %scatter_fusion.1 = f32[24,128,128]{2,1,0:T(8,128)S(1)} fusion(f32[24,128,128]{2,1,0:T(8,128)S(1)} %get-tuple-element.503, s32[128]{0:T(128)S(1)} %get-tuple-element.462, f32[128,128,128]{2,1,0:T(8,128)} %fusion.101), kind=kCustom, calls=%fused_computation.4.clone.1 | custom fusion | flops 2097152 | bytes 25166336 | tf_op jit(solution)/shard_map/while/body/eval_jaxpr/scatter-add | solution.py:101
  417.4 8.0 fusion.101
  425.4 17.1 %scatter_fusion.1 = f32[24,128,128]{2,1,0:T(8,128)S(1)} fusion(f32[24,128,128]{2,1,0:T(8,128)S(1)} %get-tuple-element.503, s32[128]{0:T(128)S(1)} %get-tuple-element.462, f32[128,128,128]{2,1,0:T(8,128)} %fusion.101), kind=kCustom, calls=%fused_computation.4.clone.1 | custom fusion | flops 2097152 | bytes 25166336 | tf_op jit(solution)/shard_map/while/body/eval_jaxpr/scatter-add | solution.py:101
  453.6 17.1 %scatter_fusion.1 = f32[24,128,128]{2,1,0:T(8,128)S(1)} fusion(f32[24,128,128]{2,1,0:T(8,128)S(1)} %get-tuple-element.503, s32[128]{0:T(128)S(1)} %get-tuple-element.462, f32[128,128,128]{2,1,0:T(8,128)} %fusion.101), kind=kCustom, calls=%fused_computation.4.clone.1 | custom fusion | flops 2097152 | bytes 25166336 | tf_op jit(solution)/shard_map/while/body/eval_jaxpr/scatter-add | solution.py:101
  485.6 38.1 %all-to-all-done.1 = f32[16,3,128,128]{3,2,1,0:T(8,128)S(1)} async-done(((f32[16,3,128,128]{3,2,1,0:T(8,128)}), f32[16,3,128,128]{3,2,1,0:T(8,128)S(1)}, u32[]{:S(2)}, u32[]{:S(2)}) %all-to-all-start.1) | async-done | bytes 3145760 | tf_op jit(solution)/shard_map/all_to_all | solution.py:112
  526.2 9.9 scatter_fusion.3
  536.1 10.8 convolution_bitcast_fusion.4
  551.6 138.9 %all-reduce.2.cloned.1.call-done = f32[128,128]{1,0:T(8,128)} async-done(((f32[128,128]{1,0:T(8,128)}), f32[128,128]{1,0:T(8,128)}) %all-reduce.2.cloned.1.call-update) | async-done | bytes 65552 | tf_op jit(solution)/shard_map/psum | solution.py:127
  691.4 255.7 %while.52 = (s32[]{:T(128)}, f32[128,128]{1,0:T(8,128)S(1)}, f32[128,128]{1,0:T(8,128)S(1)}, s32[]{:T(128)}, s32[]{:T(128)}) while((s32[]{:T(128)}, f32[128,128]{1,0:T(8,128)S(1)}, f32[128,128]{1,0:T(8,128)S(1)}, s32[]{:T(128)}, s32[]{:T(128)}) %tuple.118), condition=%wide.region_15.16_spmd.clone.clone, body=%wide.region_13.15_spmd.clone.clone.sunk | while | flops 673410 | bytes 332909 | solution.py:28
  947.9 231.7 %while.51 = (s32[]{:T(128)}, f32[128,128]{1,0:T(8,128)S(1)}, f32[128,128]{1,0:T(8,128)S(1)}, s32[]{:T(128)}, s32[]{:T(128)}) while((s32[]{:T(128)}, f32[128,128]{1,0:T(8,128)S(1)}, f32[128,128]{1,0:T(8,128)S(1)}, s32[]{:T(128)}, s32[]{:T(128)}) %tuple.121), condition=%wide.region_18.19_spmd.clone, body=%wide.region_16.18_spmd.clone.sunk | while | flops 460034 | bytes 265308 | solution.py:42
  (1355 shorter events, 481.6 us)
Async XLA Ops:
  7.2 203.1 %all-gather.2.cloned.1.call-start = ((), (), s32[]{:S(2)}) async-start(), calls=%async_computation.2 | async-start | bytes 35651584 | tf_op jit(solution)/shard_map/all_gather | solution.py:67
  10.0 468.1 %all-to-all-start = ((s32[16,1,3]{2,1,0:T(1,128)}), s32[16,1,3]{2,1,0:T(1,128)}, u32[]{:S(2)}, u32[]{:S(2)}) async-start(s32[16,1,3]{2,1,0:T(1,128)} %bitcast.12), calls=%async_computation | async-start | bytes 16384 | tf_op jit(solution)/shard_map/all_to_all | solution.py:63
  40.1 204.3 %copy-start = (s32[512]{0:T(512)S(1)}, s32[512]{0:T(512)}, u32[]{:S(2)}) copy-start(s32[512]{0:T(512)} %param.16) | copy-start | bytes 6148
  40.1 204.3 %copy-start.1 = (s32[512]{0:T(512)S(1)}, s32[512]{0:T(512)}, u32[]{:S(2)}) copy-start(s32[512]{0:T(512)} %param.15) | copy-start | bytes 6148
  478.1 45.6 %all-to-all-start.1 = ((f32[16,3,128,128]{3,2,1,0:T(8,128)}), f32[16,3,128,128]{3,2,1,0:T(8,128)S(1)}, u32[]{:S(2)}, u32[]{:S(2)}) async-start(f32[16,3,128,128]{3,2,1,0:T(8,128)} %bitcast.134), calls=%async_computation.1 | async-start | bytes 6291456 | tf_op jit(solution)/shard_map/all_to_all | solution.py:112
  483.4 207.2 %all-reduce.2.cloned.1.call-start = ((), (), s32[]{:S(2)}) async-start(), calls=%async_computation.3 | async-start | bytes 131072 | tf_op jit(solution)/shard_map/psum | solution.py:127
Sparse Core Ops, SparseCore 0:
  10.1 200.1 all-gather.1
  547.1 143.4 all-reduce.1
where the time goes:
time: 1200 us; the launch traced here: 1190 us
  matrix products  446 us (37%)
  waiting for transfers between devices  348 us (29%)
  other arithmetic  177 us (15%)
  loops' own time  98.1 us (8%)
  local copies, waits for them, and re-layouts  95.9 us (8%)
  between operations  14.2 us (1%)
  starting transfers between devices  14 us (1%)
    all_gather x1, waiting for transfers between devices, local(): shard_rows = lax.all_gather(sketch, 'dev', axis=0, tiled=True)  170 us
    psum x1, waiting for transfers between devices, local(): lax.psum(jnp.dot(normal.T, normal, precision=lax.Precision.HIGHEST), ('gr...  139 us
    dot_general x128, matrix products, column_step(): rest = target - jnp.dot(lower, row_part, precision=lax.Precision.HIGHEST)  113 us
    dot_general x128, matrix products, row_step(): jnp.dot(row_part, inverse, precision=lax.Precision.HIGHEST)  108 us
    dot_general x128, matrix products, row_step(): row_part = jnp.dot(pick, lower, precision=lax.Precision.HIGHEST)  107 us
    another operation x1, loops' own time, factor_lower(): lax.fori_loop(0, width, column_step, jnp.zeros((width, width), jnp.float32))  94 us
    scatter-add x4, other arithmetic, image_step(): return (running.at[ray_block].add(product), None)  68.2 us
    scatter-add x4, other arithmetic, normal_step(): return (running.at[col_block].add(product), None)  68.2 us
  transfers between devices with their start and end apart: 4, of which 3 were waited for; matrix products, arithmetic and copies ran while one was open for 25% of the time, Pallas kernels for 0%

commit v1 on v0

v1 whole, which is shorter than its diff:
```python
import functools

import jax
import jax.numpy as jnp
from jax import lax
from jax.experimental import pallas as pl
from jax.experimental.pallas import tpu as pltpu
from jax.sharding import PartitionSpec as P

CAP = 3
RB_DEV = 32
BLK = 128
SIDE = 4
GROUP = SIDE * SIDE
SLOTS = GROUP * CAP
gram_shift = 0.001

MESH = pl.DeviceIdType.MESH
SMEM = pltpu.SMEM
VMEM = pltpu.VMEM
f32 = jnp.float32
bf16 = jnp.bfloat16


def vm():
    return pl.BlockSpec(memory_space=VMEM)


def sm():
    return pl.BlockSpec(memory_space=SMEM)


def hbm():
    return pl.BlockSpec(memory_space=pl.ANY)


def prep_kernel(block_count, touched, home, ray, col, req, slot, table, count):
    ntouch = touched.shape[0]
    ntiles = ray.shape[0]

    def init_count(i, c):
        count[i] = 0
        return c

    def init_req(i, c):
        req[i] = -1
        return c

    def init_table(i, c):
        table[i] = ntiles
        return c

    lax.fori_loop(0, GROUP, init_count, 0, unroll=True)
    lax.fori_loop(0, SLOTS, init_req, 0, unroll=True)
    lax.fori_loop(0, RB_DEV * ntouch, init_table, 0, unroll=16)

    def place(j, c):
        stored = home[touched[j]]
        holder = lax.rem(lax.div(stored, block_count), GROUP)
        n = count[holder]
        count[holder] = n + 1
        s = holder * CAP + n
        slot[j] = s
        req[s] = lax.rem(stored, block_count)
        return c

    lax.fori_loop(0, ntouch, place, 0)

    def fill(t, c):
        table[ray[t] * ntouch + col[t]] = t
        return c

    lax.fori_loop(0, ntiles, fill, 0, unroll=16)


OFFSETS = [(dx, dz) for dx in range(SIDE) for dz in range(SIDE) if (dx, dz) != (0, 0)]


def peer_of(me, dx, dz):
    x, z = lax.div(me, SIDE), lax.rem(me, SIDE)
    return lax.rem(x + dx, SIDE) * SIDE + lax.rem(z + dz, SIDE)


def plane_barrier(me):
    barrier = pltpu.get_barrier_semaphore()
    for dx, dz in OFFSETS:
        pl.semaphore_signal(
            barrier, inc=1, device_id={"dev": peer_of(me, dx, dz)}, device_id_type=MESH
        )
    pl.semaphore_wait(barrier, GROUP - 1)


def fetch_kernel(
    req, sketch, got, incoming, ask, asked, asked_s, packed, send, recv, asend, arecv, lsem
):
    me = lax.axis_index("dev")
    lane = lax.broadcasted_iota(jnp.int32, (8, BLK), 1)
    for p in range(GROUP):
        ask[p] = jnp.where(
            lane == 0, req[3 * p], jnp.where(lane == 1, req[3 * p + 1], req[3 * p + 2])
        )
    plane_barrier(me)
    asks = []
    for i, (dx, dz) in enumerate(OFFSETS):
        p = peer_of(me, dx, dz)
        c = pltpu.make_async_remote_copy(
            src_ref=ask.at[p],
            dst_ref=asked.at[me],
            send_sem=asend.at[i],
            recv_sem=arecv.at[i],
            device_id={"dev": p},
            device_id_type=MESH,
        )
        c.start()
        asks.append(c)
    asked[me] = ask[me]
    for c in asks:
        c.wait()
    local = pltpu.make_async_copy(asked, asked_s, lsem)
    local.start()
    local.wait()

    copies = []
    for i, (dx, dz) in enumerate(OFFSETS):
        p = peer_of(me, dx, dz)
        for k in range(CAP):
            packed[p, k] = sketch[jnp.maximum(asked_s[p, 0, k], 0)]
        c = pltpu.make_async_remote_copy(
            src_ref=packed.at[p],
            dst_ref=got.at[me],
            send_sem=send.at[i],
            recv_sem=recv.at[i],
            device_id={"dev": p},
            device_id_type=MESH,
        )
        c.start()
        copies.append(c)
    for k in range(CAP):
        got[me, k] = sketch[jnp.maximum(asked_s[me, 0, k], 0)]
    for p in range(GROUP):
        for k in range(CAP):
            incoming[CAP * p + k] = asked_s[p, 0, k]
    for c in copies:
        c.wait()


def exchange_kernel(out, arrived, send, recv):
    me = lax.axis_index("dev")
    plane_barrier(me)
    copies = []
    for i, (dx, dz) in enumerate(OFFSETS):
        p = peer_of(me, dx, dz)
        c = pltpu.make_async_remote_copy(
            src_ref=out.at[p],
            dst_ref=arrived.at[me],
            send_sem=send.at[i],
            recv_sem=recv.at[i],
            device_id={"dev": p},
            device_id_type=MESH,
        )
        c.start()
        copies.append(c)
    arrived[me] = out[me]
    for c in copies:
        c.wait()


def apply_kernel(ntouch, table, slot, tiles, xs, out, held, xc, images_t, sem):
    ntiles = tiles.shape[0]
    chunks = 8
    step = ntiles // chunks
    loads = []
    for i in range(chunks):
        c = pltpu.make_async_copy(
            tiles.at[pl.ds(i * step, step)], held.at[pl.ds(i * step, step)], sem.at[i]
        )
        c.start()
        loads.append(c)
    held[ntiles] = jnp.zeros((BLK, BLK), bf16)
    for c in range(ntouch):
        xc[pl.ds(c * BLK, BLK), :] = xs[slot[c]]
    for c in loads:
        c.wait()

    per = 2

    def image_step(g, carry):
        rows = [
            jnp.concatenate(
                [held[table[(g * per + i) * ntouch + c]] for c in range(ntouch)], axis=1
            )
            for i in range(per)
        ]
        lhs = jnp.concatenate(rows, axis=0)
        got = jnp.dot(lhs, xc[...], preferred_element_type=f32)
        start = pl.multiple_of(g * (per * BLK), per * BLK)
        images_t[:, pl.ds(start, per * BLK)] = got.T.astype(bf16)
        return carry

    lax.fori_loop(0, RB_DEV // per, image_step, 0)

    def normal_step(g, carry):
        cols = [
            jnp.concatenate(
                [held[table[r * ntouch + g * 2 + i]] for r in range(RB_DEV)], axis=0
            )
            for i in range(2)
        ]
        rhs = jnp.concatenate(cols, axis=1)
        part = jnp.dot(images_t[...], rhs, preferred_element_type=f32)
        for i in range(2):
            out[slot[g * 2 + i]] = part[:, i * BLK : (i + 1) * BLK].T.astype(bf16)
        return carry

    lax.fori_loop(0, ntouch // 2, normal_step, 0)


def split(value):
    high = value.astype(bf16)
    return high, (value - high.astype(f32)).astype(bf16)


def gather_kernel(incoming, arrived, normal, gram):
    normal[...] = jnp.zeros_like(normal)

    def add(s, c):
        row = incoming[s]

        @pl.when(row >= 0)
        def _():
            normal[row] = normal[row] + arrived[s].astype(f32)

        return c

    lax.fori_loop(0, SLOTS, add, 0)

    gram[...] = jnp.zeros_like(gram)
    blocks = normal.shape[0]
    per = 8

    def accumulate(g, c):
        rows = normal[pl.ds(g * per, per)].reshape(per * BLK, BLK)
        high, low = split(rows)
        both = jnp.concatenate([high, low], axis=1)
        part = lax.dot_general(
            high, both, (((0,), (0,)), ((), ())), preferred_element_type=f32
        )
        gram[...] += part
        return c

    lax.fori_loop(0, blocks // per, accumulate, 0)


def reduce_kernel(voxels, both, total, mine, first, part, second, s1, r1, s2, r2, s3, r3):
    me = lax.axis_index("dev")
    grp = lax.axis_index("grp")
    groups = lax.axis_size("grp")
    cross = both[:, BLK:]
    mine[...] = (both[:, :BLK] + cross + cross.T).reshape(mine.shape)

    barrier = pltpu.get_barrier_semaphore()
    for dx, dz in OFFSETS:
        pl.semaphore_signal(
            barrier, inc=1, device_id={"dev": peer_of(me, dx, dz)}, device_id_type=MESH
        )
    for o in range(1, groups):
        pl.semaphore_signal(
            barrier, inc=1, device_id={"grp": lax.rem(grp + o, groups)}, device_id_type=MESH
        )
    pl.semaphore_wait(barrier, GROUP - 1 + groups - 1)

    copies = []
    for i, (dx, dz) in enumerate(OFFSETS):
        p = peer_of(me, dx, dz)
        c = pltpu.make_async_remote_copy(
            src_ref=mine.at[p],
            dst_ref=first.at[me],
            send_sem=s1.at[i],
            recv_sem=r1.at[i],
            device_id={"dev": p},
            device_id_type=MESH,
        )
        c.start()
        copies.append(c)
    first[me] = mine[me]
    for c in copies:
        c.wait()
    chunk = first[0]
    for p in range(1, GROUP):
        chunk = chunk + first[p]
    part[...] = chunk

    copies = []
    for o in range(1, groups):
        g = lax.rem(grp + o, groups)
        c = pltpu.make_async_remote_copy(
            src_ref=part,
            dst_ref=second.at[grp],
            send_sem=s2.at[o - 1],
            recv_sem=r2.at[o - 1],
            device_id={"grp": g},
            device_id_type=MESH,
        )
        c.start()
        copies.append(c)
    second[grp] = chunk
    for c in copies:
        c.wait()
    chunk = second[0]
    for g in range(1, groups):
        chunk = chunk + second[g]
    total[me] = chunk / voxels

    copies = []
    for i, (dx, dz) in enumerate(OFFSETS):
        p = peer_of(me, dx, dz)
        c = pltpu.make_async_remote_copy(
            src_ref=total.at[me],
            dst_ref=total.at[me],
            send_sem=s3.at[i],
            recv_sem=r3.at[i],
            device_id={"dev": p},
            device_id_type=MESH,
        )
        c.start()
        copies.append(c)
    for c in copies:
        c.wait()


def factor(gram):
    n = gram.shape[0]
    bands = n // 8
    row_id = lax.broadcasted_iota(jnp.int32, (8, n), 0)
    lane_id = lax.broadcasted_iota(jnp.int32, (8, n), 1)
    g = [gram[8 * b : 8 * b + 8, :] for b in range(bands)]
    w = [jnp.where(lane_id == row_id + 8 * b, 1.0, 0.0).astype(f32) for b in range(bands)]
    r_bands, w_bands = [], []
    for b in range(bands):
        r_out = jnp.zeros((8, n), f32)
        w_out = jnp.zeros((8, n), f32)
        for k in range(8):
            j = 8 * b + k
            g_row = jnp.broadcast_to(g[b][k : k + 1, :], (8, n))
            w_row = jnp.broadcast_to(w[b][k : k + 1, :], (8, n))
            pivot = jnp.broadcast_to(g_row[:, j : j + 1], (8, n))
            scale = 1.0 / pivot
            g_s = g_row * scale
            w_s = w_row * scale
            for t in range(b, bands):
                factor_t = jnp.broadcast_to(g[t][:, j : j + 1], (8, n))
                if t == b:
                    if k == 7:
                        continue
                    factor_t = jnp.where(row_id > k, factor_t, 0.0)
                g[t] = g[t] - factor_t * g_s
                w[t] = w[t] - factor_t * w_s
            root = jnp.sqrt(pivot)
            r_out = jnp.where(row_id == k, g_s * root, r_out)
            w_out = jnp.where(row_id == k, w_s * root, w_out)
        r_bands.append(jnp.where(lane_id >= row_id + 8 * b, r_out, 0.0))
        w_bands.append(w_out)
    return jnp.concatenate(r_bands, axis=0), jnp.concatenate(w_bands, axis=0)


def basis_kernel(total, normal, basis, r_factor, inverse):
    @pl.when(pl.program_id(0) == 0)
    def _():
        rows = lax.broadcasted_iota(jnp.int32, (BLK, BLK), 0)
        cols = lax.broadcasted_iota(jnp.int32, (BLK, BLK), 1)
        gram = total[...].reshape(BLK, BLK)
        gram = gram + jnp.where(rows == cols, gram_shift, 0.0).astype(f32)
        r_value, lower_inverse = factor(gram)
        r_factor[...] = r_value
        high, low = split(lower_inverse.T)
        inverse[:BLK, :BLK] = high
        inverse[BLK:, :BLK] = high
        inverse[:BLK, BLK:] = low
        inverse[BLK:, BLK:] = jnp.zeros_like(low)

    high, low = split(normal[...])
    got = jnp.dot(
        jnp.concatenate([high, low], axis=1), inverse[...], preferred_element_type=f32
    )
    basis[...] = got[:, :BLK] + got[:, BLK:]


def local(tiles, tile_ray, tile_col, touched, home, sketch):
    block_count = sketch.shape[0] // BLK
    ntouch = touched.shape[0]
    ntiles = tiles.shape[0]
    groups = lax.axis_size("grp")
    i32 = jnp.int32
    dma = pltpu.SemaphoreType.DMA
    peers = GROUP - 1

    req, slot, table = pl.pallas_call(
        functools.partial(prep_kernel, block_count),
        out_shape=(
            jax.ShapeDtypeStruct((SLOTS,), i32),
            jax.ShapeDtypeStruct((ntouch,), i32),
            jax.ShapeDtypeStruct((RB_DEV * ntouch,), i32),
        ),
        in_specs=[sm()] * 4,
        out_specs=(sm(),) * 3,
        scratch_shapes=[SMEM((GROUP,), i32)],
        name="prep",
    )(touched, home, tile_ray, tile_col)

    got, incoming = pl.pallas_call(
        fetch_kernel,
        out_shape=(
            jax.ShapeDtypeStruct((GROUP, CAP, BLK, BLK), bf16),
            jax.ShapeDtypeStruct((SLOTS,), i32),
        ),
        in_specs=[sm(), vm()],
        out_specs=(vm(), sm()),
        scratch_shapes=[
            VMEM((GROUP, 8, BLK), i32),
            VMEM((GROUP, 8, BLK), i32),
            SMEM((GROUP, 8, BLK), i32),
            VMEM((GROUP, CAP, BLK, BLK), bf16),
            dma((peers,)),
            dma((peers,)),
            dma((peers,)),
            dma((peers,)),
            dma,
        ],
        compiler_params=pltpu.CompilerParams(collective_id=1, has_side_effects=True),
        name="fetch",
    )(req, sketch.reshape(block_count, BLK, BLK))

    out = pl.pallas_call(
        functools.partial(apply_kernel, ntouch),
        out_shape=jax.ShapeDtypeStruct((SLOTS, BLK, BLK), bf16),
        in_specs=[sm(), sm(), hbm(), vm()],
        out_specs=vm(),
        scratch_shapes=[
            VMEM((ntiles + 1, BLK, BLK), bf16),
            VMEM((ntouch * BLK, BLK), bf16),
            VMEM((BLK, RB_DEV * BLK), bf16),
            dma((8,)),
        ],
        compiler_params=pltpu.CompilerParams(vmem_limit_bytes=48 << 20),
        name="apply",
    )(table, slot, tiles, got.reshape(SLOTS, BLK, BLK))

    arrived = pl.pallas_call(
        exchange_kernel,
        out_shape=jax.ShapeDtypeStruct((GROUP, CAP, BLK, BLK), bf16),
        in_specs=[vm()],
        out_specs=vm(),
        scratch_shapes=[dma((peers,)), dma((peers,))],
        compiler_params=pltpu.CompilerParams(collective_id=2, has_side_effects=True),
        name="exchange",
    )(out.reshape(GROUP, CAP, BLK, BLK))

    normal, both = pl.pallas_call(
        gather_kernel,
        out_shape=(
            jax.ShapeDtypeStruct((block_count, BLK, BLK), f32),
            jax.ShapeDtypeStruct((BLK, 2 * BLK), f32),
        ),
        in_specs=[sm(), vm()],
        out_specs=(vm(), vm()),
        name="gather",
    )(incoming, arrived.reshape(SLOTS, BLK, BLK))

    voxels = float(sketch.shape[0] * groups * GROUP)
    total = pl.pallas_call(
        functools.partial(reduce_kernel, voxels),
        out_shape=jax.ShapeDtypeStruct((GROUP, BLK // GROUP, BLK), f32),
        in_specs=[vm()],
        out_specs=vm(),
        scratch_shapes=[
            VMEM((GROUP, BLK // GROUP, BLK), f32),
            VMEM((GROUP, BLK // GROUP, BLK), f32),
            VMEM((BLK // GROUP, BLK), f32),
            VMEM((groups, BLK // GROUP, BLK), f32),
            dma((peers,)),
            dma((peers,)),
            dma((groups - 1,)),
            dma((groups - 1,)),
            dma((peers,)),
            dma((peers,)),
        ],
        compiler_params=pltpu.CompilerParams(collective_id=3, has_side_effects=True),
        name="reduce",
    )(both)

    rows = block_count * BLK
    step = rows // 8
    basis, r_factor = pl.pallas_call(
        basis_kernel,
        grid=(8,),
        out_shape=(
            jax.ShapeDtypeStruct((rows, BLK), f32),
            jax.ShapeDtypeStruct((BLK, BLK), f32),
        ),
        in_specs=[
            pl.BlockSpec((GROUP, BLK // GROUP, BLK), lambda i: (0, 0, 0)),
            pl.BlockSpec((step, BLK), lambda i: (i, 0)),
        ],
        out_specs=(
            pl.BlockSpec((step, BLK), lambda i: (i, 0)),
            pl.BlockSpec((BLK, BLK), lambda i: (0, 0)),
        ),
        scratch_shapes=[VMEM((2 * BLK, 2 * BLK), bf16)],
        name="basis",
    )(total, normal.reshape(rows, BLK))
    return (basis, r_factor)


def solution(mesh):
    in_specs = (
        P(("grp", "dev"), None, None),
        P(("grp", "dev")),
        P(("grp", "dev")),
        P(("grp", "dev")),
        P(),
        P(("grp", "dev"), None),
    )
    out_specs = (P(("grp", "dev"), None), P())
    return jax.shard_map(local, mesh=mesh, in_specs=in_specs, out_specs=out_specs, check_vma=False)
```

time: 1200 us -> 145 us (0.12)
  matrix products: 446 us -> 0 us
  waiting for transfers between devices: 348 us -> 0 us
  other arithmetic: 177 us -> 0 us
  Pallas kernels: 0 us -> 142 us
  loops' own time: 98.1 us -> 0 us
  local copies, waits for them, and re-layouts: 95.9 us -> 2.55 us
  starting transfers between devices: 14 us -> 0 us
  between operations: 14.2 us -> 0.72 us
    dot_general x650 -> x0, matrix products: 446 us -> none  [the longest x128 113 us: column_step(): rest = target - jnp.dot(lower, row_part, precision=lax.Precision.HIGHEST)]
    all_gather x1 -> x0, waiting for transfers between devices: 170 us -> none  [local(): shard_rows = lax.all_gather(sketch, 'dev', axis=0, tiled=True)]
    scatter-add x9 -> x0, other arithmetic: 146 us -> none  [the longest x4 68.2 us: image_step(): return (running.at[ray_block].add(product), None)]
    pallas_call x0 -> x7, Pallas kernels: none -> 142 us  [the longest x1 33.9 us: local(): pl.pallas_call(fetch_kernel, out_shape=(jax.ShapeDtypeStruct((GROUP, CAP,...]
    psum x1 -> x0, waiting for transfers between devices: 139 us -> none  [local(): lax.psum(jnp.dot(normal.T, normal, precision=lax.Precision.HIGHEST), ('gr...]
    another operation x4 -> x0, loops' own time: 98.1 us -> none  [the longest x1 94 us: factor_lower(): lax.fori_loop(0, width, column_step, jnp.zeros((width, width), jnp.float32))]
    gather x9 -> x0, local copies, waits for them, and re-layouts: 57.5 us -> none  [the longest x1 32.7 us: local(): jnp.take(shard_rows, jnp.clip(wanted, 0, length - 1).reshape(-1), axis=0)]
    all_to_all x2 -> x0, waiting for transfers between devices: 38.1 us -> none  [the longest x1 38.1 us: local(): lax.all_to_all(outgoing.reshape(group_size, CAP, tile_size, width), 'dev'...]
  transfers between devices with their start and end apart: 4 -> 0, of which waited for: 3 -> 0; matrix products, arithmetic and copies ran while one was open for 25% -> 0% of each run, Pallas kernels for 0% -> 0%
where the time goes in v1:
time: 145 us
  Pallas kernels  142 us (98%)
  local copies, waits for them, and re-layouts  2.55 us (2%)
    pallas_call x1, Pallas kernels, local(): pl.pallas_call(fetch_kernel, out_shape=(jax.ShapeDtypeStruct((GROUP, CAP,...  33.9 us
    pallas_call x1, Pallas kernels, local(): pl.pallas_call(functools.partial(reduce_kernel, voxels), out_shape=jax.Sh...  25.1 us
    pallas_call x1, Pallas kernels, local(): pl.pallas_call(basis_kernel, grid=(8,), out_shape=(jax.ShapeDtypeStruct((...  24.7 us
    pallas_call x1, Pallas kernels, local(): pl.pallas_call(exchange_kernel, out_shape=jax.ShapeDtypeStruct((GROUP, CA...  24.6 us
    pallas_call x1, Pallas kernels, local(): pl.pallas_call(functools.partial(apply_kernel, ntouch), out_shape=jax.Sha...  22.9 us
    pallas_call x1, Pallas kernels, local(): pl.pallas_call(gather_kernel, out_shape=(jax.ShapeDtypeStruct((block_coun...  6.42 us
    pallas_call x1, Pallas kernels, local(): pl.pallas_call(functools.partial(prep_kernel, block_count), out_shape=(ja...  4.07 us

profile of v1, /device:TPU:1, one launch (start us, length us, event | category | flops | bytes accessed | tf_op | source)
XLA Modules:
  0.0 144.9 jit_solution(16379892114079868928)
XLA Ops:
  0.6 4.1 %prep.1 = (s32[48]{0:T(128)}, s32[24]{0:T(128)}, s32[768]{0:T(1024)}) custom-call(s32[24]{0:T(128)} %touched.1, s32[8192]{0:T(1024)} %home.1, s32[512]{0:T(512)} %ray.1, s32[512]{0:T(512)} %col.1), custom_call_target="tpu_custom_call" | custom-call | tf_op jit(solution)/shard_map/prep/pallas_call | solution.py:397
  4.7 0.0 copy-start.2
  4.7 0.0 copy-start.3
  4.7 33.9 %fetch.1 = (bf16[16,3,128,128]{3,2,1,0:T(8,128)(2,1)}, s32[48]{0:T(128)}) custom-call(s32[48]{0:T(128)} %get-tuple-element.9.req, bf16[64,128,128]{2,1,0:T(8,128)(2,1)} %bitcast.9), custom_call_target="tpu_custom_call" | custom-call | tf_op jit(solution)/shard_map/fetch/pallas_call | solution.py:410
  38.6 0.0 copy-done.2
  38.6 0.0 copy-done.3
  38.6 0.0 copy-start.1
  38.7 1.4 copy-done.1
  40.1 22.9 %apply.1 = bf16[48,128,128]{2,1,0:T(8,128)(2,1)S(1)} custom-call(s32[768]{0:T(1024)S(1)} %copy-done.2, s32[24]{0:T(128)S(1)} %copy-done.3, bf16[512,128,128]{2,1,0:T(8,128)(2,1)} %tiles.1, bf16[48,128,128]{2,1,0:T(8,128)(2,1)S(1)} %bitcast.6), custom_call_target="tpu_custom_call" | custom-call | tf_op jit(solution)/shard_map/apply/pallas_call | solution.py:433
  62.9 0.0 copy-start
  62.9 1.1 copy-done
  64.1 24.6 %exchange.1 = bf16[16,3,128,128]{3,2,1,0:T(8,128)(2,1)} custom-call(bf16[16,3,128,128]{3,2,1,0:T(8,128)(2,1)} %bitcast.5), custom_call_target="tpu_custom_call" | custom-call | tf_op jit(solution)/shard_map/exchange/pallas_call | solution.py:448
  88.7 6.4 %gather.1 = (f32[64,128,128]{2,1,0:T(8,128)}, f32[128,256]{1,0:T(8,128)}) custom-call(s32[48]{0:T(128)} %get-tuple-element.10.incoming, bf16[48,128,128]{2,1,0:T(8,128)(2,1)} %bitcast.7), custom_call_target="tpu_custom_call" | custom-call | tf_op jit(solution)/shard_map/gather/pallas_call | solution.py:458
  95.1 25.1 %reduce.1.total = f32[16,8,128]{2,1,0:T(8,128)} custom-call(f32[128,256]{1,0:T(8,128)} %get-tuple-element.14.both), custom_call_target="tpu_custom_call" | custom-call | tf_op jit(solution)/shard_map/reduce/pallas_call | solution.py:470
  120.2 24.7 %basis.1 = (f32[8192,128]{1,0:T(8,128)}, f32[128,128]{1,0:T(8,128)}) custom-call(f32[16,8,128]{2,1,0:T(8,128)} %reduce.1.total, f32[8192,128]{1,0:T(8,128)} %bitcast.8), custom_call_target="tpu_custom_call" | custom-call | tf_op jit(solution)/shard_map/basis/pallas_call | solution.py:493
Async XLA Ops:
  4.7 33.9 %copy-start.2 = (s32[768]{0:T(1024)S(1)}, s32[768]{0:T(1024)}, u32[]{:S(2)}) copy-start(s32[768]{0:T(1024)} %get-tuple-element.11.table) | copy-start | bytes 9220
  4.7 33.9 %copy-start.3 = (s32[24]{0:T(128)S(1)}, s32[24]{0:T(128)}, u32[]{:S(2)}) copy-start(s32[24]{0:T(128)} %get-tuple-element.12.slot) | copy-start | bytes 292
  38.6 1.4 copy-start.1
  62.9 1.1 copy-start

commit v2 on v1

v2 whole, which is shorter than its diff:
```python
import functools

import jax
import jax.numpy as jnp
from jax import lax
from jax.experimental import pallas as pl
from jax.experimental.pallas import tpu as pltpu
from jax.sharding import PartitionSpec as P

CAP = 3
RB_DEV = 32
BLK = 128
SIDE = 4
GROUP = SIDE * SIDE
CHUNKS = 8
SLOTS = GROUP * CAP
gram_shift = 0.001
LEVELS = 32767.0
TINY = 1e-30

MESH = pl.DeviceIdType.MESH
SMEM = pltpu.SMEM
VMEM = pltpu.VMEM
f32 = jnp.float32
bf16 = jnp.bfloat16


def vm():
    return pl.BlockSpec(memory_space=VMEM)


def sm():
    return pl.BlockSpec(memory_space=SMEM)


def hbm():
    return pl.BlockSpec(memory_space=pl.ANY)


OFFSETS = [(dx, dz) for dx in range(SIDE) for dz in range(SIDE) if (dx, dz) != (0, 0)]


def peer_of(me, dx, dz):
    x, z = lax.div(me, SIDE), lax.rem(me, SIDE)
    return lax.rem(x + dx, SIDE) * SIDE + lax.rem(z + dz, SIDE)


def plane_barrier(me):
    barrier = pltpu.get_barrier_semaphore()
    for dx, dz in OFFSETS:
        pl.semaphore_signal(
            barrier, inc=1, device_id={"dev": peer_of(me, dx, dz)}, device_id_type=MESH
        )
    pl.semaphore_wait(barrier, GROUP - 1)


def fetch_kernel(
    block_count,
    touched,
    home,
    sketch_in,
    got,
    incoming,
    slot,
    sketch,
    ask,
    asked,
    asked_s,
    packed,
    send,
    recv,
    asend,
    arecv,
    lsem,
    ssem,
):
    me = lax.axis_index("dev")
    whole = pltpu.make_async_copy(sketch_in, sketch, ssem)
    whole.start()
    barrier = pltpu.get_barrier_semaphore()
    for dx, dz in OFFSETS:
        pl.semaphore_signal(
            barrier, inc=1, device_id={"dev": peer_of(me, dx, dz)}, device_id_type=MESH
        )

    lane = lax.broadcasted_iota(jnp.int32, (8, BLK), 1)
    wanted = jnp.full((8, BLK), -1, jnp.int32)
    holders = []
    for j in range(touched.shape[0]):
        stored = home[touched[j]]
        holder = lax.rem(lax.div(stored, block_count), GROUP)
        n = jnp.int32(0)
        for earlier in holders:
            n = n + (earlier == holder).astype(jnp.int32)
        holders.append(holder)
        s = holder * CAP + n
        slot[j] = s
        wanted = jnp.where(lane == s, lax.rem(stored, block_count), wanted)
    ask[...] = wanted
    asked[me] = wanted

    pl.semaphore_wait(barrier, GROUP - 1)
    asks = []
    for i, (dx, dz) in enumerate(OFFSETS):
        c = pltpu.make_async_remote_copy(
            src_ref=ask,
            dst_ref=asked.at[me],
            send_sem=asend.at[i],
            recv_sem=arecv.at[i],
            device_id={"dev": peer_of(me, dx, dz)},
            device_id_type=MESH,
        )
        c.start()
        asks.append(c)
    whole.wait()
    for c in asks:
        c.wait()
    local = pltpu.make_async_copy(asked, asked_s, lsem)
    local.start()
    local.wait()

    copies = []
    for i, (dx, dz) in enumerate(OFFSETS):
        p = peer_of(me, dx, dz)
        for k in range(CAP):
            packed[p, k] = sketch[jnp.maximum(asked_s[p, 0, CAP * me + k], 0)]
        c = pltpu.make_async_remote_copy(
            src_ref=packed.at[p],
            dst_ref=got.at[me],
            send_sem=send.at[i],
            recv_sem=recv.at[i],
            device_id={"dev": p},
            device_id_type=MESH,
        )
        c.start()
        copies.append(c)
    for k in range(CAP):
        got[me, k] = sketch[jnp.maximum(asked_s[me, 0, CAP * me + k], 0)]
    for p in range(GROUP):
        for k in range(CAP):
            incoming[CAP * p + k] = asked_s[p, 0, CAP * me + k]
    for c in copies:
        c.wait()


def exchange_kernel(out, scales, arrived, arrived_scales, send, recv, send2, recv2):
    me = lax.axis_index("dev")
    plane_barrier(me)
    copies = []
    for i, (dx, dz) in enumerate(OFFSETS):
        p = peer_of(me, dx, dz)
        for src, dst, s, r in (
            (scales, arrived_scales, send2, recv2),
            (out, arrived, send, recv),
        ):
            c = pltpu.make_async_remote_copy(
                src_ref=src.at[p],
                dst_ref=dst.at[me],
                send_sem=s.at[i],
                recv_sem=r.at[i],
                device_id={"dev": p},
                device_id_type=MESH,
            )
            c.start()
            copies.append(c)
    arrived[me] = out[me]
    arrived_scales[me] = scales[me]
    for c in copies:
        c.wait()


def apply_kernel(
    ntouch, ray, col, slot, tiles, xs, out, scales, held, xc, images_t, table, sem
):
    ntiles = tiles.shape[0]
    chunks = 8
    step = ntiles // chunks
    loads = []
    for i in range(chunks):
        c = pltpu.make_async_copy(
            tiles.at[pl.ds(i * step, step)], held.at[pl.ds(i * step, step)], sem.at[i]
        )
        c.start()
        loads.append(c)
    held[ntiles] = jnp.zeros((BLK, BLK), bf16)
    for c in range(ntouch):
        xc[pl.ds(c * BLK, BLK), :] = xs[slot[c]]

    def init(i, c):
        table[i] = ntiles
        return c

    def fill(t, c):
        table[ray[t] * ntouch + col[t]] = t
        return c

    lax.fori_loop(0, RB_DEV * ntouch, init, 0, unroll=16)
    lax.fori_loop(0, ntiles, fill, 0, unroll=16)
    for c in loads:
        c.wait()

    per = 4

    def image_step(g, carry):
        rows = [
            jnp.concatenate(
                [held[table[(g * per + i) * ntouch + c]] for c in range(ntouch)], axis=1
            )
            for i in range(per)
        ]
        lhs = jnp.concatenate(rows, axis=0)
        got = jnp.dot(lhs, xc[...], preferred_element_type=f32)
        start = pl.multiple_of(g * (per * BLK), per * BLK)
        images_t[:, pl.ds(start, per * BLK)] = got.T.astype(bf16)
        return carry

    lax.fori_loop(0, RB_DEV // per, image_step, 0)

    def normal_step(g, carry):
        cols = [
            jnp.concatenate(
                [held[table[r * ntouch + g * 2 + i]] for r in range(RB_DEV)], axis=0
            )
            for i in range(2)
        ]
        rhs = jnp.concatenate(cols, axis=1)
        part = jnp.dot(images_t[...], rhs, preferred_element_type=f32)
        for i in range(2):
            s = slot[g * 2 + i]
            block = part[:, i * BLK : (i + 1) * BLK].T
            top = jnp.maximum(jnp.max(jnp.abs(block), axis=0, keepdims=True), TINY)
            code = jnp.round(block * (LEVELS / top))
            out[s] = code.astype(jnp.int32).astype(jnp.int16)
            scales[lax.div(s, CAP), pl.ds(lax.rem(s, CAP), 1), :] = top * (1.0 / LEVELS)
        return carry

    lax.fori_loop(0, ntouch // 2, normal_step, 0)


def split(value):
    high = value.astype(bf16)
    return high, (value - high.astype(f32)).astype(bf16)


def gather_kernel(incoming, arrived, scales, normal):
    normal[...] = jnp.zeros_like(normal)

    def add(s, c):
        row = incoming[s]

        @pl.when(row >= 0)
        def _():
            scale = scales[lax.div(s, CAP), pl.ds(lax.rem(s, CAP), 1), :]
            code = arrived[s].astype(jnp.int32).astype(f32)
            normal[row] = normal[row] + code * scale

        return c

    lax.fori_loop(0, SLOTS, add, 0)


def reduce_kernel(
    voxels, normal, total, held, both, mine, first, part, second, s1, r1, s2, r2, s3, r3, lsem
):
    me = lax.axis_index("dev")
    grp = lax.axis_index("grp")
    groups = lax.axis_size("grp")
    blocks = held.shape[0]
    per = blocks // CHUNKS
    loads = []
    for i in range(CHUNKS):
        c = pltpu.make_async_copy(
            normal.at[pl.ds(i * per, per)], held.at[pl.ds(i * per, per)], lsem.at[i]
        )
        c.start()
        loads.append(c)

    barrier = pltpu.get_barrier_semaphore()
    for dx, dz in OFFSETS:
        pl.semaphore_signal(
            barrier, inc=1, device_id={"dev": peer_of(me, dx, dz)}, device_id_type=MESH
        )
    for o in range(1, groups):
        pl.semaphore_signal(
            barrier, inc=1, device_id={"grp": lax.rem(grp + o, groups)}, device_id_type=MESH
        )

    both[...] = jnp.zeros_like(both)
    for c in loads:
        c.wait()

    def accumulate(g, c):
        rows = held[pl.ds(g * per, per)].reshape(per * BLK, BLK)
        high, low = split(rows)
        pair = jnp.concatenate([high, low], axis=1)
        both[...] += lax.dot_general(
            high, pair, (((0,), (0,)), ((), ())), preferred_element_type=f32
        )
        return c

    lax.fori_loop(0, CHUNKS, accumulate, 0)
    cross = both[:, BLK:]
    mine[...] = (both[:, :BLK] + cross + cross.T).reshape(mine.shape)
    pl.semaphore_wait(barrier, GROUP - 1 + groups - 1)

    copies = []
    for i, (dx, dz) in enumerate(OFFSETS):
        p = peer_of(me, dx, dz)
        c = pltpu.make_async_remote_copy(
            src_ref=mine.at[p],
            dst_ref=first.at[me],
            send_sem=s1.at[i],
            recv_sem=r1.at[i],
            device_id={"dev": p},
            device_id_type=MESH,
        )
        c.start()
        copies.append(c)
    first[me] = mine[me]
    for c in copies:
        c.wait()
    chunk = first[0]
    for p in range(1, GROUP):
        chunk = chunk + first[p]
    part[...] = chunk

    copies = []
    for o in range(1, groups):
        g = lax.rem(grp + o, groups)
        c = pltpu.make_async_remote_copy(
            src_ref=part,
            dst_ref=second.at[grp],
            send_sem=s2.at[o - 1],
            recv_sem=r2.at[o - 1],
            device_id={"grp": g},
            device_id_type=MESH,
        )
        c.start()
        copies.append(c)
    second[grp] = chunk
    for c in copies:
        c.wait()
    chunk = second[0]
    for g in range(1, groups):
        chunk = chunk + second[g]
    total[me] = chunk / voxels

    copies = []
    for i, (dx, dz) in enumerate(OFFSETS):
        p = peer_of(me, dx, dz)
        c = pltpu.make_async_remote_copy(
            src_ref=total.at[me],
            dst_ref=total.at[me],
            send_sem=s3.at[i],
            recv_sem=r3.at[i],
            device_id={"dev": p},
            device_id_type=MESH,
        )
        c.start()
        copies.append(c)
    for c in copies:
        c.wait()


def factor(gram):
    n = gram.shape[0]
    bands = n // 8
    shape = (8, n)
    row_id = lax.broadcasted_iota(jnp.int32, shape, 0)
    lane_id = lax.broadcasted_iota(jnp.int32, shape, 1)
    g = [gram[8 * b : 8 * b + 8, :] for b in range(bands)]
    w = [jnp.where(lane_id == row_id + 8 * b, 1.0, 0.0).astype(f32) for b in range(bands)]
    r_bands, w_bands = [], []
    for b in range(bands):
        cols = [
            [jnp.broadcast_to(g[t][:, 8 * b + k : 8 * b + k + 1], shape) for k in range(8)]
            for t in range(b, bands)
        ]
        cols[0] = [jnp.where(lane_id < n, c, 0.0) for c in cols[0]]
        pivots = jnp.ones(shape, f32)
        for k in range(8):
            pivot = jnp.broadcast_to(cols[0][k][k : k + 1, :], shape)
            scale = 1.0 / pivot
            pivots = jnp.where(row_id == k, pivot, pivots)
            g_s = jnp.broadcast_to(g[b][k : k + 1, :], shape) * scale
            w_s = jnp.broadcast_to(w[b][k : k + 1, :], shape) * scale
            c_s = {
                j: jnp.broadcast_to(cols[0][j][k : k + 1, :], shape) * scale
                for j in range(k + 1, 8)
            }
            for t in range(b, bands):
                own = cols[t - b]
                f = own[k]
                if t == b:
                    if k == 7:
                        continue
                    f = jnp.where(row_id > k, f, 0.0)
                for j in range(k + 1, 8):
                    own[j] = own[j] - f * c_s[j]
                g[t] = g[t] - f * g_s
                w[t] = w[t] - f * w_s
        root = 1.0 / jnp.sqrt(pivots)
        r_bands.append(jnp.where(lane_id >= row_id + 8 * b, g[b] * root, 0.0))
        w_bands.append(w[b] * root)
    return jnp.concatenate(r_bands, axis=0), jnp.concatenate(w_bands, axis=0)


def basis_kernel(total, normal, basis, r_factor, inverse):
    @pl.when(pl.program_id(0) == 0)
    def _():
        rows = lax.broadcasted_iota(jnp.int32, (BLK, BLK), 0)
        cols = lax.broadcasted_iota(jnp.int32, (BLK, BLK), 1)
        gram = total[...].reshape(BLK, BLK)
        gram = gram + jnp.where(rows == cols, gram_shift, 0.0).astype(f32)
        r_value, lower_inverse = factor(gram)
        r_factor[...] = r_value
        high, low = split(lower_inverse.T)
        inverse[:BLK, :BLK] = high
        inverse[BLK:, :BLK] = high
        inverse[:BLK, BLK:] = low
        inverse[BLK:, BLK:] = jnp.zeros_like(low)

    high, low = split(normal[...])
    got = jnp.dot(
        jnp.concatenate([high, low], axis=1), inverse[...], preferred_element_type=f32
    )
    basis[...] = got[:, :BLK] + got[:, BLK:]


def local(tiles, tile_ray, tile_col, touched, home, sketch):
    block_count = sketch.shape[0] // BLK
    ntouch = touched.shape[0]
    ntiles = tiles.shape[0]
    groups = lax.axis_size("grp")
    i32 = jnp.int32
    dma = pltpu.SemaphoreType.DMA
    peers = GROUP - 1

    got, incoming, slot = pl.pallas_call(
        functools.partial(fetch_kernel, block_count),
        out_shape=(
            jax.ShapeDtypeStruct((GROUP, CAP, BLK, BLK), bf16),
            jax.ShapeDtypeStruct((SLOTS,), i32),
            jax.ShapeDtypeStruct((ntouch,), i32),
        ),
        in_specs=[sm(), sm(), hbm()],
        out_specs=(vm(), sm(), sm()),
        scratch_shapes=[
            VMEM((block_count, BLK, BLK), bf16),
            VMEM((8, BLK), i32),
            VMEM((GROUP, 8, BLK), i32),
            SMEM((GROUP, 8, BLK), i32),
            VMEM((GROUP, CAP, BLK, BLK), bf16),
            dma((peers,)),
            dma((peers,)),
            dma((peers,)),
            dma((peers,)),
            dma,
            dma,
        ],
        compiler_params=pltpu.CompilerParams(collective_id=1, has_side_effects=True),
        name="fetch",
    )(touched, home, sketch.reshape(block_count, BLK, BLK))

    out, scales = pl.pallas_call(
        functools.partial(apply_kernel, ntouch),
        out_shape=(
            jax.ShapeDtypeStruct((SLOTS, BLK, BLK), jnp.int16),
            jax.ShapeDtypeStruct((GROUP, 8, BLK), f32),
        ),
        in_specs=[sm(), sm(), sm(), hbm(), vm()],
        out_specs=(vm(), vm()),
        scratch_shapes=[
            VMEM((ntiles + 1, BLK, BLK), bf16),
            VMEM((ntouch * BLK, BLK), bf16),
            VMEM((BLK, RB_DEV * BLK), bf16),
            SMEM((RB_DEV * ntouch,), i32),
            dma((8,)),
        ],
        compiler_params=pltpu.CompilerParams(vmem_limit_bytes=48 << 20),
        name="apply",
    )(tile_ray, tile_col, slot, tiles, got.reshape(SLOTS, BLK, BLK))

    arrived, arrived_scales = pl.pallas_call(
        exchange_kernel,
        out_shape=(
            jax.ShapeDtypeStruct((GROUP, CAP, BLK, BLK), jnp.int16),
            jax.ShapeDtypeStruct((GROUP, 8, BLK), f32),
        ),
        in_specs=[vm(), vm()],
        out_specs=(vm(), vm()),
        scratch_shapes=[dma((peers,))] * 4,
        compiler_params=pltpu.CompilerParams(collective_id=2, has_side_effects=True),
        name="exchange",
    )(out.reshape(GROUP, CAP, BLK, BLK), scales)

    normal = pl.pallas_call(
        gather_kernel,
        out_shape=jax.ShapeDtypeStruct((block_count, BLK, BLK), f32),
        in_specs=[sm(), vm(), vm()],
        out_specs=vm(),
        name="gather",
    )(incoming, arrived.reshape(SLOTS, BLK, BLK), arrived_scales)

    voxels = float(sketch.shape[0] * groups * GROUP)
    total = pl.pallas_call(
        functools.partial(reduce_kernel, voxels),
        out_shape=jax.ShapeDtypeStruct((GROUP, BLK // GROUP, BLK), f32),
        in_specs=[hbm()],
        out_specs=vm(),
        scratch_shapes=[
            VMEM((block_count, BLK, BLK), f32),
            VMEM((BLK, 2 * BLK), f32),
            VMEM((GROUP, BLK // GROUP, BLK), f32),
            VMEM((GROUP, BLK // GROUP, BLK), f32),
            VMEM((BLK // GROUP, BLK), f32),
            VMEM((groups, BLK // GROUP, BLK), f32),
            dma((peers,)),
            dma((peers,)),
            dma((groups - 1,)),
            dma((groups - 1,)),
            dma((peers,)),
            dma((peers,)),
            dma((CHUNKS,)),
        ],
        compiler_params=pltpu.CompilerParams(collective_id=3, has_side_effects=True),
        name="reduce",
    )(normal)

    rows = block_count * BLK
    step = rows // 8
    basis, r_factor = pl.pallas_call(
        basis_kernel,
        grid=(8,),
        out_shape=(
            jax.ShapeDtypeStruct((rows, BLK), f32),
            jax.ShapeDtypeStruct((BLK, BLK), f32),
        ),
        in_specs=[
            pl.BlockSpec((GROUP, BLK // GROUP, BLK), lambda i: (0, 0, 0)),
            pl.BlockSpec((step, BLK), lambda i: (i, 0)),
        ],
        out_specs=(
            pl.BlockSpec((step, BLK), lambda i: (i, 0)),
            pl.BlockSpec((BLK, BLK), lambda i: (0, 0)),
        ),
        scratch_shapes=[VMEM((2 * BLK, 2 * BLK), bf16)],
        name="basis",
    )(total, normal.reshape(rows, BLK))
    return (basis, r_factor)


def solution(mesh):
    in_specs = (
        P(("grp", "dev"), None, None),
        P(("grp", "dev")),
        P(("grp", "dev")),
        P(("grp", "dev")),
        P(),
        P(("grp", "dev"), None),
    )
    out_specs = (P(("grp", "dev"), None), P())
    return jax.shard_map(local, mesh=mesh, in_specs=in_specs, out_specs=out_specs, check_vma=False)
```

time: 145 us -> 126 us (0.87)
  Pallas kernels: 142 us -> 121 us
    pallas_call x1, Pallas kernels: 24.7 us -> 10.7 us  [local(): pl.pallas_call(basis_kernel, grid=(8,), out_shape=(jax.ShapeDtypeStruct((...]
    pallas_call x5 -> x4, Pallas kernels: 91.8 us -> 85.1 us  [the longest x1 33.5 us: local(): pl.pallas_call(functools.partial(fetch_kernel, block_count), out_shape=(j...]
    unnamed x8 -> x12, local copies, waits for them, and re-layouts: 2.55 us -> 3.84 us
where the time goes in v2:
time: 126 us
  Pallas kernels  121 us (96%)
  local copies, waits for them, and re-layouts  3.84 us (3%)
    pallas_call x1, Pallas kernels, local(): pl.pallas_call(functools.partial(fetch_kernel, block_count), out_shape=(j...  33.5 us
    pallas_call x1, Pallas kernels, local(): pl.pallas_call(exchange_kernel, out_shape=(jax.ShapeDtypeStruct((GROUP, C...  25.6 us
    pallas_call x1, Pallas kernels, local(): pl.pallas_call(functools.partial(reduce_kernel, voxels), out_shape=jax.Sh...  25.2 us
    pallas_call x1, Pallas kernels, local(): pl.pallas_call(functools.partial(apply_kernel, ntouch), out_shape=(jax.Sh...  21.5 us
    pallas_call x1, Pallas kernels, local(): pl.pallas_call(basis_kernel, grid=(8,), out_shape=(jax.ShapeDtypeStruct((...  10.7 us
    pallas_call x1, Pallas kernels, local(): pl.pallas_call(gather_kernel, out_shape=jax.ShapeDtypeStruct((block_count...  4.52 us
    unnamed x12, local copies, waits for them, and re-layouts  3.84 us

profile of v2, /device:TPU:1, one launch (start us, length us, event | category | flops | bytes accessed | tf_op | source)
XLA Modules:
  0.0 125.6 jit_solution(15250020866477818030)
XLA Ops:
  0.6 0.0 copy-start.4
  0.6 0.0 copy-start.3
  0.7 33.5 %fetch.1 = (bf16[16,3,128,128]{3,2,1,0:T(8,128)(2,1)}, s32[48]{0:T(128)}, s32[24]{0:T(128)}) custom-call(s32[24]{0:T(128)} %touched.1, s32[8192]{0:T(1024)} %home.1, bf16[64,128,128]{2,1,0:T(8,128)(2,1)} %bitcast.8), custom_call_target="tpu_custom_call" | custom-call | tf_op jit(solution)/shard_map/fetch/pallas_call | solution.py:439
  34.1 0.0 copy-done.4
  34.2 0.0 copy-done.3
  34.2 0.0 copy-start
  34.2 1.4 %copy-done = bf16[16,3,128,128]{3,2,1,0:T(8,128)(2,1)S(1)} copy-done((bf16[16,3,128,128]{3,2,1,0:T(8,128)(2,1)S(1)}, bf16[16,3,128,128]{3,2,1,0:T(8,128)(2,1)}, u32[]{:S(2)}) %copy-start) | copy-done | bytes 1572888
  35.6 0.0 copy-start.5
  35.6 0.7 copy-done.5
  36.2 21.5 %apply.1 = (s16[48,128,128]{2,1,0:T(8,128)(2,1)S(1)}, f32[16,8,128]{2,1,0:T(8,128)S(1)}) custom-call(s32[512]{0:T(512)S(1)} %copy-done.3, s32[512]{0:T(512)S(1)} %copy-done.4, s32[24]{0:T(128)S(1)} %copy-done.5, bf16[512,128,128]{2,1,0:T(8,128)(2,1)} %tiles.1, bf16[48,128,128]{2,1,0:T(8,128)(2,1)S(1)} %bitcast.5), custom_call_target="tpu_custom_call" | custom-call | tf_op jit(solution)/shard_map/apply/pallas_call | solution.py:465
  57.7 0.0 copy-start.1
  57.7 1.1 copy-done.1
  58.9 0.0 copy-start.2
  58.9 0.6 copy-done.2
  59.5 25.6 %exchange.1 = (s16[16,3,128,128]{3,2,1,0:T(8,128)(2,1)}, f32[16,8,128]{2,1,0:T(8,128)}) custom-call(s16[16,3,128,128]{3,2,1,0:T(8,128)(2,1)} %bitcast.6, f32[16,8,128]{2,1,0:T(8,128)} %copy-done.2), custom_call_target="tpu_custom_call" | custom-call | tf_op jit(solution)/shard_map/exchange/pallas_call | solution.py:484
  85.1 4.5 %gather.1.normal = f32[64,128,128]{2,1,0:T(8,128)} custom-call(s32[48]{0:T(128)} %get-tuple-element.9.incoming, s16[48,128,128]{2,1,0:T(8,128)(2,1)} %bitcast.9, f32[16,8,128]{2,1,0:T(8,128)} %get-tuple-element.15.scales), custom_call_target="tpu_custom_call" | custom-call | tf_op jit(solution)/shard_map/gather/pallas_call | solution.py:497
  89.7 25.2 %reduce.1.total = f32[16,8,128]{2,1,0:T(8,128)} custom-call(f32[64,128,128]{2,1,0:T(8,128)} %gather.1.normal), custom_call_target="tpu_custom_call" | custom-call | tf_op jit(solution)/shard_map/reduce/pallas_call | solution.py:506
  114.8 10.7 %basis.1 = (f32[8192,128]{1,0:T(8,128)}, f32[128,128]{1,0:T(8,128)}) custom-call(f32[16,8,128]{2,1,0:T(8,128)} %reduce.1.total, f32[8192,128]{1,0:T(8,128)} %bitcast.7), custom_call_target="tpu_custom_call" | custom-call | tf_op jit(solution)/shard_map/basis/pallas_call | solution.py:532
Async XLA Ops:
  0.6 33.5 %copy-start.4 = (s32[512]{0:T(512)S(1)}, s32[512]{0:T(512)}, u32[]{:S(2)}) copy-start(s32[512]{0:T(512)} %col.1) | copy-start | bytes 6148
  0.6 33.5 %copy-start.3 = (s32[512]{0:T(512)S(1)}, s32[512]{0:T(512)}, u32[]{:S(2)}) copy-start(s32[512]{0:T(512)} %ray.1) | copy-start | bytes 6148
  34.2 1.4 %copy-start = (bf16[16,3,128,128]{3,2,1,0:T(8,128)(2,1)S(1)}, bf16[16,3,128,128]{3,2,1,0:T(8,128)(2,1)}, u32[]{:S(2)}) copy-start(bf16[16,3,128,128]{3,2,1,0:T(8,128)(2,1)} %get-tuple-element.11) | copy-start | bytes 4718596
  35.6 0.7 copy-start.5
  57.7 1.1 copy-start.1
  58.9 0.6 copy-start.2

commit v3 on v2

--- a/solution.py
+++ b/solution.py
@@ -13,6 +13,7 @@
 SIDE = 4
 GROUP = SIDE * SIDE
 CHUNKS = 8
+PER = 8
 SLOTS = GROUP * CAP
 gram_shift = 0.001
 LEVELS = 32767.0
@@ -37,7 +38,10 @@
     return pl.BlockSpec(memory_space=pl.ANY)
 
 
-OFFSETS = [(dx, dz) for dx in range(SIDE) for dz in range(SIDE) if (dx, dz) != (0, 0)]
+OFFSETS = sorted(
+    [(dx, dz) for dx in range(SIDE) for dz in range(SIDE) if (dx, dz) != (0, 0)],
+    key=lambda o: (-(min(o[0], SIDE - o[0]) + min(o[1], SIDE - o[1])), o),
+)
 
 
 def peer_of(me, dx, dz):
@@ -45,56 +49,86 @@
     return lax.rem(x + dx, SIDE) * SIDE + lax.rem(z + dz, SIDE)
 
 
-def plane_barrier(me):
+def cycle_kernel(
+    block_count,
+    touched,
+    home,
+    ray,
+    col,
+    sketch_in,
+    tiles_in,
+    arrived,
+    arrived_scales,
+    incoming,
+    sketch,
+    held,
+    ask,
+    asked,
+    asked_s,
+    index,
+    index_s,
+    place_s,
+    packed,
+    got,
+    xc,
+    images_t,
+    codes,
+    code_scales,
+    out,
+    scales,
+    asend,
+    arecv,
+    send,
+    recv,
+    send2,
+    recv2,
+    send3,
+    recv3,
+    tsem,
+    ssem,
+    lsem,
+    isem,
+):
+    me = lax.axis_index("dev")
+    ntouch = touched.shape[0]
+    ntiles = ray.shape[0]
+    i32 = jnp.int32
+    whole = pltpu.make_async_copy(sketch_in, sketch, ssem)
+    whole.start()
+    step = ntiles // CHUNKS
+    loads = []
+    for i in range(CHUNKS):
+        c = pltpu.make_async_copy(
+            tiles_in.at[pl.ds(i * step, step)], held.at[pl.ds(i * step, step)], tsem.at[i]
+        )
+        c.start()
+        loads.append(c)
     barrier = pltpu.get_barrier_semaphore()
     for dx, dz in OFFSETS:
         pl.semaphore_signal(
             barrier, inc=1, device_id={"dev": peer_of(me, dx, dz)}, device_id_type=MESH
         )
-    pl.semaphore_wait(barrier, GROUP - 1)
-
-
-def fetch_kernel(
-    block_count,
-    touched,
-    home,
-    sketch_in,
-    got,
-    incoming,
-    slot,
-    sketch,
-    ask,
-    asked,
-    asked_s,
-    packed,
-    send,
-    recv,
-    asend,
-    arecv,
-    lsem,
-    ssem,
-):
-    me = lax.axis_index("dev")
-    whole = pltpu.make_async_copy(sketch_in, sketch, ssem)
-    whole.start()
-    barrier = pltpu.get_barrier_semaphore()
-    for dx, dz in OFFSETS:
-        pl.semaphore_signal(
-            barrier, inc=1, device_id={"dev": peer_of(me, dx, dz)}, device_id_type=MESH
-        )
-
-    lane = lax.broadcasted_iota(jnp.int32, (8, BLK), 1)
-    wanted = jnp.full((8, BLK), -1, jnp.int32)
-    holders = []
-    for j in range(touched.shape[0]):
+
+    for q, (dx, dz) in enumerate(OFFSETS + [(0, 0)]):
+        place_s[dx * SIDE + dz] = q
+    x, z = lax.div(me, SIDE), lax.rem(me, SIDE)
+    lane = lax.broadcasted_iota(i32, (8, BLK), 1)
+    row = lax.broadcasted_iota(i32, (8, BLK), 0)
+    wanted = jnp.full((8, BLK), -1, i32)
+    holders, slots, keys = [], [], []
+    for j in range(ntouch):
         stored = home[touched[j]]
         holder = lax.rem(lax.div(stored, block_count), GROUP)
-        n = jnp.int32(0)
+        n = i32(0)
         for earlier in holders:
-            n = n + (earlier == holder).astype(jnp.int32)
+            n = n + (earlier == holder).astype(i32)
+        n = jnp.minimum(n, CAP - 1)
         holders.append(holder)
         s = holder * CAP + n
-        slot[j] = s
+        slots.append(s)
+        hx, hz = lax.div(holder, SIDE), lax.rem(holder, SIDE)
+        far = lax.rem(hx - x + SIDE, SIDE) * SIDE + lax.rem(hz - z + SIDE, SIDE)
+        keys.append(place_s[far] * CAP + n)
         wanted = jnp.where(lane == s, lax.rem(stored, block_count), wanted)
     ask[...] = wanted
     asked[me] = wanted
@@ -112,6 +146,35 @@
         )
         c.start()
         asks.append(c)
+
+    order = jnp.zeros((8, BLK), i32)
+    for j in range(ntouch):
+        rank = i32(0)
+        for k in range(ntouch):
+            if k != j:
+                rank = rank + (keys[k] < keys[j]).astype(i32)
+        order = jnp.where((row == 0) & (lane == rank), j, order)
+        order = jnp.where((row == 1) & (lane == keys[j]), rank, order)
+    index[pl.ds(RB_DEV, 8), :] = order
+
+    bands = RB_DEV // 8
+    pairs = [
+        jnp.where(lane < ntouch, (row + 8 * b) * ntouch + lane, -1) for b in range(bands)
+    ]
+
+    def place(t, table):
+        pair = ray[t] * ntouch + col[t]
+        return tuple(jnp.where(p == pair, t, v) for p, v in zip(pairs, table))
+
+    table = lax.fori_loop(
+        0, ntiles, place, (jnp.full((8, BLK), ntiles, i32),) * bands, unroll=8
+    )
+    for b in range(bands):
+        index[pl.ds(8 * b, 8), :] = table[b]
+    tables = pltpu.make_async_copy(index, index_s, isem)
+    tables.start()
+    held[ntiles] = jnp.zeros((BLK, BLK), bf16)
+
     whole.wait()
     for c in asks:
         c.wait()
@@ -139,102 +202,80 @@
     for p in range(GROUP):
         for k in range(CAP):
             incoming[CAP * p + k] = asked_s[p, 0, CAP * me + k]
+    tables.wait()
+    for c in loads:
+        c.wait()
     for c in copies:
         c.wait()
 
-
-def exchange_kernel(out, scales, arrived, arrived_scales, send, recv, send2, recv2):
-    me = lax.axis_index("dev")
-    plane_barrier(me)
+    for c in range(ntouch):
+        holder = holders[c]
+        xc[pl.ds(c * BLK, BLK), :] = got[holder, slots[c] - CAP * holder]
+
+    def image_step(g, carry):
+        rows = [
+            jnp.concatenate(
+                [held[index_s[g * PER + i, c]] for c in range(ntouch)], axis=1
+            )
+            for i in range(PER)
+        ]
+        lhs = jnp.concatenate(rows, axis=0)
+        image = jnp.dot(lhs, xc[...], preferred_element_type=f32)
+        start = pl.multiple_of(g * (PER * BLK), PER * BLK)
+        images_t[:, pl.ds(start, PER * BLK)] = image.T.astype(bf16)
+        return carry
+
+    lax.fori_loop(0, RB_DEV // PER, image_step, 0)
+
+    def normal_step(g, carry):
+        cols = []
+        for i in range(2):
+            c = index_s[RB_DEV, 2 * g + i]
+            cols.append(
+                jnp.concatenate([held[index_s[r, c]] for r in range(RB_DEV)], axis=0)
+            )
+        rhs = jnp.concatenate(cols, axis=1)
+        part = jnp.dot(images_t[...], rhs, preferred_element_type=f32)
+        for i in range(2):
+            block = part[:, i * BLK : (i + 1) * BLK].T
+            top = jnp.maximum(jnp.max(jnp.abs(block), axis=0, keepdims=True), TINY)
+            code = jnp.round(block * (LEVELS / top))
+            codes[2 * g + i] = code.astype(i32).astype(jnp.int16)
+            code_scales[pl.ds(2 * g + i, 1), :] = top * (1.0 / LEVELS)
+        return carry
+
     copies = []
-    for i, (dx, dz) in enumerate(OFFSETS):
-        p = peer_of(me, dx, dz)
-        for src, dst, s, r in (
+    done = 0
+    for q in range(GROUP - 1):
+        until = -(-min(ntouch, CAP * (q + 1)) // 2)
+        if until > done:
+            lax.fori_loop(done, until, normal_step, 0)
+            done = until
+        p = peer_of(me, *OFFSETS[q])
+        for k in range(CAP):
+            at = index_s[RB_DEV + 1, CAP * q + k]
+            out[p, k] = codes[at]
+            scales[p, pl.ds(k, 1), :] = code_scales[pl.ds(at, 1), :]
+        for src, dst, ss, rs in (
             (scales, arrived_scales, send2, recv2),
-            (out, arrived, send, recv),
+            (out, arrived, send3, recv3),
         ):
             c = pltpu.make_async_remote_copy(
                 src_ref=src.at[p],
                 dst_ref=dst.at[me],
-                send_sem=s.at[i],
-                recv_sem=r.at[i],
+                send_sem=ss.at[q],
+                recv_sem=rs.at[q],
                 device_id={"dev": p},
                 device_id_type=MESH,
             )
             c.start()
             copies.append(c)
-    arrived[me] = out[me]
-    arrived_scales[me] = scales[me]
+    for k in range(CAP):
+        at = index_s[RB_DEV + 1, CAP * (GROUP - 1) + k]
+        arrived[me, k] = codes[at]
+        arrived_scales[me, pl.ds(k, 1), :] = code_scales[pl.ds(at, 1), :]
     for c in copies:
         c.wait()
-
-
-def apply_kernel(
-    ntouch, ray, col, slot, tiles, xs, out, scales, held, xc, images_t, table, sem
-):
-    ntiles = tiles.shape[0]
-    chunks = 8
-    step = ntiles // chunks
-    loads = []
-    for i in range(chunks):
-        c = pltpu.make_async_copy(
-            tiles.at[pl.ds(i * step, step)], held.at[pl.ds(i * step, step)], sem.at[i]
-        )
-        c.start()
-        loads.append(c)
-    held[ntiles] = jnp.zeros((BLK, BLK), bf16)
-    for c in range(ntouch):
-        xc[pl.ds(c * BLK, BLK), :] = xs[slot[c]]
-
-    def init(i, c):
-        table[i] = ntiles
-        return c
-
-    def fill(t, c):
-        table[ray[t] * ntouch + col[t]] = t
-        return c
-
-    lax.fori_loop(0, RB_DEV * ntouch, init, 0, unroll=16)
-    lax.fori_loop(0, ntiles, fill, 0, unroll=16)
-    for c in loads:
-        c.wait()
-
-    per = 4
-
-    def image_step(g, carry):
-        rows = [
-            jnp.concatenate(
-                [held[table[(g * per + i) * ntouch + c]] for c in range(ntouch)], axis=1
-            )
-            for i in range(per)
-        ]
-        lhs = jnp.concatenate(rows, axis=0)
-        got = jnp.dot(lhs, xc[...], preferred_element_type=f32)
-        start = pl.multiple_of(g * (per * BLK), per * BLK)
-        images_t[:, pl.ds(start, per * BLK)] = got.T.astype(bf16)
-        return carry
-
-    lax.fori_loop(0, RB_DEV // per, image_step, 0)
-
-    def normal_step(g, carry):
-        cols = [
-            jnp.concatenate(
-                [held[table[r * ntouch + g * 2 + i]] for r in range(RB_DEV)], axis=0
-            )
-            for i in range(2)
-        ]
-        rhs = jnp.concatenate(cols, axis=1)
-        part = jnp.dot(images_t[...], rhs, preferred_element_type=f32)
-        for i in range(2):
-            s = slot[g * 2 + i]
-            block = part[:, i * BLK : (i + 1) * BLK].T
-            top = jnp.maximum(jnp.max(jnp.abs(block), axis=0, keepdims=True), TINY)
-            code = jnp.round(block * (LEVELS / top))
-            out[s] = code.astype(jnp.int32).astype(jnp.int16)
-            scales[lax.div(s, CAP), pl.ds(lax.rem(s, CAP), 1), :] = top * (1.0 / LEVELS)
-        return carry
-
-    lax.fori_loop(0, ntouch // 2, normal_step, 0)
 
 
 def split(value):
@@ -436,63 +477,38 @@
     dma = pltpu.SemaphoreType.DMA
     peers = GROUP - 1
 
-    got, incoming, slot = pl.pallas_call(
-        functools.partial(fetch_kernel, block_count),
+    arrived, arrived_scales, incoming = pl.pallas_call(
+        functools.partial(cycle_kernel, block_count),
         out_shape=(
-            jax.ShapeDtypeStruct((GROUP, CAP, BLK, BLK), bf16),
+            jax.ShapeDtypeStruct((GROUP, CAP, BLK, BLK), jnp.int16),
+            jax.ShapeDtypeStruct((GROUP, 8, BLK), f32),
             jax.ShapeDtypeStruct((SLOTS,), i32),
-            jax.ShapeDtypeStruct((ntouch,), i32),
         ),
-        in_specs=[sm(), sm(), hbm()],
-        out_specs=(vm(), sm(), sm()),
+        in_specs=[sm(), sm(), sm(), sm(), hbm(), hbm()],
+        out_specs=(vm(), vm(), sm()),
         scratch_shapes=[
             VMEM((block_count, BLK, BLK), bf16),
+            VMEM((ntiles + 1, BLK, BLK), bf16),
             VMEM((8, BLK), i32),
             VMEM((GROUP, 8, BLK), i32),
             SMEM((GROUP, 8, BLK), i32),
+            VMEM((RB_DEV + 8, BLK), i32),
+            SMEM((RB_DEV + 8, BLK), i32),
+            SMEM((GROUP,), i32),
             VMEM((GROUP, CAP, BLK, BLK), bf16),
-            dma((peers,)),
-            dma((peers,)),
-            dma((peers,)),
-            dma((peers,)),
-            dma,
-            dma,
-        ],
-        compiler_params=pltpu.CompilerParams(collective_id=1, has_side_effects=True),
-        name="fetch",
-    )(touched, home, sketch.reshape(block_count, BLK, BLK))
-
-    out, scales = pl.pallas_call(
-        functools.partial(apply_kernel, ntouch),
-        out_shape=(
-            jax.ShapeDtypeStruct((SLOTS, BLK, BLK), jnp.int16),
-            jax.ShapeDtypeStruct((GROUP, 8, BLK), f32),
-        ),
-        in_specs=[sm(), sm(), sm(), hbm(), vm()],
-        out_specs=(vm(), vm()),
-        scratch_shapes=[
-            VMEM((ntiles + 1, BLK, BLK), bf16),
+            VMEM((GROUP, CAP, BLK, BLK), bf16),
             VMEM((ntouch * BLK, BLK), bf16),
             VMEM((BLK, RB_DEV * BLK), bf16),
-            SMEM((RB_DEV * ntouch,), i32),
-            dma((8,)),
-        ],
-        compiler_params=pltpu.CompilerParams(vmem_limit_bytes=48 << 20),
-        name="apply",
-    )(tile_ray, tile_col, slot, tiles, got.reshape(SLOTS, BLK, BLK))
-
-    arrived, arrived_scales = pl.pallas_call(
-        exchange_kernel,
-        out_shape=(
-            jax.ShapeDtypeStruct((GROUP, CAP, BLK, BLK), jnp.int16),
-            jax.ShapeDtypeStruct((GROUP, 8, BLK), f32),
-        ),
-        in_specs=[vm(), vm()],
-        out_specs=(vm(), vm()),
-        scratch_shapes=[dma((peers,))] * 4,
-        compiler_params=pltpu.CompilerParams(collective_id=2, has_side_effects=True),
-        name="exchange",
-    )(out.reshape(GROUP, CAP, BLK, BLK), scales)
+            VMEM((ntouch, BLK, BLK), jnp.int16),
+            VMEM((ntouch, BLK), f32),
+            VMEM((GROUP, CAP, BLK, BLK), jnp.int16),
+            VMEM((GROUP, 8, BLK), f32),
+        ]
+        + [dma((peers,))] * 8
+        + [dma((CHUNKS,)), dma, dma, dma],
+        compiler_params=pltpu.CompilerParams(collective_id=1, has_side_effects=True),
+        name="cycle",
+    )(touched, home, tile_ray, tile_col, sketch.reshape(block_count, BLK, BLK), tiles)
 
     normal = pl.pallas_call(
         gather_kernel,

time: 126 us -> 104 us (0.83)
  Pallas kernels: 121 us -> 103 us
  local copies, waits for them, and re-layouts: 3.84 us -> 0 us
    pallas_call x3 -> x1, Pallas kernels: 80.6 us -> 65.6 us  [local(): pl.pallas_call(functools.partial(cycle_kernel, block_count), out_shape=(j...]
    unnamed x12 -> x0, local copies, waits for them, and re-layouts: 3.84 us -> none
    pallas_call x1, Pallas kernels: 25.2 us -> 22.1 us  [local(): pl.pallas_call(functools.partial(reduce_kernel, voxels), out_shape=jax.Sh...]
where the time goes in v3:
time: 104 us
  Pallas kernels  103 us (99%)
    pallas_call x1, Pallas kernels, local(): pl.pallas_call(functools.partial(cycle_kernel, block_count), out_shape=(j...  65.6 us
    pallas_call x1, Pallas kernels, local(): pl.pallas_call(functools.partial(reduce_kernel, voxels), out_shape=jax.Sh...  22.1 us
    pallas_call x1, Pallas kernels, local(): pl.pallas_call(basis_kernel, grid=(8,), out_shape=(jax.ShapeDtypeStruct((...  10.7 us
    pallas_call x1, Pallas kernels, local(): pl.pallas_call(gather_kernel, out_shape=jax.ShapeDtypeStruct((block_count...  4.61 us

profile of v3, /device:TPU:1, one launch (start us, length us, event | category | flops | bytes accessed | tf_op | source)
XLA Modules:
  0.0 103.7 jit_solution(9192573185563031837)
XLA Ops:
  0.6 65.6 %cycle.1 = (s16[16,3,128,128]{3,2,1,0:T(8,128)(2,1)}, f32[16,8,128]{2,1,0:T(8,128)}, s32[48]{0:T(128)}) custom-call(s32[24]{0:T(128)} %touched.1, s32[8192]{0:T(1024)} %home.1, s32[512]{0:T(512)} %ray.1, s32[512]{0:T(512)} %col.1, bf16[64,128,128]{2,1,0:T(8,128)(2,1)} %bitcast.4, bf16[512,128,128]{2,1,0:T(8,128)(2,1)} %tiles_in.1), custom_call_target="tpu_custom_call" | custom-call | tf_op jit(solution)/shard_map/cycle/pallas_call | solution.py:480
  66.2 4.6 %gather.1.normal = f32[64,128,128]{2,1,0:T(8,128)} custom-call(s32[48]{0:T(128)} %get-tuple-element.5.incoming, s16[48,128,128]{2,1,0:T(8,128)(2,1)} %bitcast.5, f32[16,8,128]{2,1,0:T(8,128)} %get-tuple-element.7.scales), custom_call_target="tpu_custom_call" | custom-call | tf_op jit(solution)/shard_map/gather/pallas_call | solution.py:513
  70.8 22.1 %reduce.1.total = f32[16,8,128]{2,1,0:T(8,128)} custom-call(f32[64,128,128]{2,1,0:T(8,128)} %gather.1.normal), custom_call_target="tpu_custom_call" | custom-call | tf_op jit(solution)/shard_map/reduce/pallas_call | solution.py:522
  93.0 10.7 %basis.1 = (f32[8192,128]{1,0:T(8,128)}, f32[128,128]{1,0:T(8,128)}) custom-call(f32[16,8,128]{2,1,0:T(8,128)} %reduce.1.total, f32[8192,128]{1,0:T(8,128)} %bitcast.3), custom_call_target="tpu_custom_call" | custom-call | tf_op jit(solution)/shard_map/basis/pallas_call | solution.py:548

commit v4 on v3

--- a/solution.py
+++ b/solution.py
@@ -14,6 +14,11 @@
 GROUP = SIDE * SIDE
 CHUNKS = 8
 PER = 8
+STAGES = (12, 14, 16)
+ORDER = RB_DEV
+PLACE = RB_DEV + 1
+COMING = RB_DEV + 2
+SLOT = RB_DEV + 3
 SLOTS = GROUP * CAP
 gram_shift = 0.001
 LEVELS = 32767.0
@@ -68,9 +73,13 @@
     index,
     index_s,
     place_s,
+    coming_s,
     packed,
-    got,
+    got_0,
+    got_1,
+    got_2,
     xc,
+    sums,
     images_t,
     codes,
     code_scales,
@@ -111,11 +120,13 @@
 
     for q, (dx, dz) in enumerate(OFFSETS + [(0, 0)]):
         place_s[dx * SIDE + dz] = q
+        back = (SIDE - dx) % SIDE * SIDE + (SIDE - dz) % SIDE
+        coming_s[back] = (q + 1) % GROUP
     x, z = lax.div(me, SIDE), lax.rem(me, SIDE)
     lane = lax.broadcasted_iota(i32, (8, BLK), 1)
     row = lax.broadcasted_iota(i32, (8, BLK), 0)
     wanted = jnp.full((8, BLK), -1, i32)
-    holders, slots, keys = [], [], []
+    holders, keys, arrivals = [], [], []
     for j in range(ntouch):
         stored = home[touched[j]]
         holder = lax.rem(lax.div(stored, block_count), GROUP)
@@ -125,10 +136,10 @@
         n = jnp.minimum(n, CAP - 1)
         holders.append(holder)
         s = holder * CAP + n
-        slots.append(s)
         hx, hz = lax.div(holder, SIDE), lax.rem(holder, SIDE)
         far = lax.rem(hx - x + SIDE, SIDE) * SIDE + lax.rem(hz - z + SIDE, SIDE)
         keys.append(place_s[far] * CAP + n)
+        arrivals.append(coming_s[far] * CAP + n)
         wanted = jnp.where(lane == s, lax.rem(stored, block_count), wanted)
     ask[...] = wanted
     asked[me] = wanted
@@ -155,6 +166,12 @@
                 rank = rank + (keys[k] < keys[j]).astype(i32)
         order = jnp.where((row == 0) & (lane == rank), j, order)
         order = jnp.where((row == 1) & (lane == keys[j]), rank, order)
+        rank = i32(0)
+        for k in range(ntouch):
+            if k != j:
+                rank = rank + (arrivals[k] < arrivals[j]).astype(i32)
+        order = jnp.where((row == 2) & (lane == rank), j, order)
+        order = jnp.where((row == 3) & (lane == j), arrivals[j], order)
     index[pl.ds(RB_DEV, 8), :] = order
 
     bands = RB_DEV // 8
@@ -182,14 +199,17 @@
     local.start()
     local.wait()
 
+    got = (got_0, got_1, got_2)
     copies = []
     for i, (dx, dz) in enumerate(OFFSETS):
         p = peer_of(me, dx, dz)
+        stage = sum(i + 1 >= owners for owners in STAGES)
+        first = (0, *STAGES)[stage]
         for k in range(CAP):
             packed[p, k] = sketch[jnp.maximum(asked_s[p, 0, CAP * me + k], 0)]
         c = pltpu.make_async_remote_copy(
             src_ref=packed.at[p],
-            dst_ref=got.at[me],
+            dst_ref=got[stage].at[pl.ds(CAP * (i + 1 - first), CAP)],
             send_sem=send.at[i],
             recv_sem=recv.at[i],
             device_id={"dev": p},
@@ -198,39 +218,58 @@
         c.start()
         copies.append(c)
     for k in range(CAP):
-        got[me, k] = sketch[jnp.maximum(asked_s[me, 0, CAP * me + k], 0)]
+        got_0[k] = sketch[jnp.maximum(asked_s[me, 0, CAP * me + k], 0)]
     for p in range(GROUP):
         for k in range(CAP):
             incoming[CAP * p + k] = asked_s[p, 0, CAP * me + k]
     tables.wait()
     for c in loads:
         c.wait()
+
+    received = 0
+    begin = 0
+    for owners in STAGES:
+        for c in copies[received : owners - 1]:
+            c.wait_recv()
+        received = owners - 1
+        end = max(begin, CAP * owners - (SLOTS - ntouch))
+        cols = [index_s[COMING, i] for i in range(begin, end)]
+        for i, c in enumerate(cols):
+            at = index_s[SLOT, c]
+            block = got_0[jnp.minimum(at, CAP * STAGES[0] - 1)]
+            for stage in range(1, len(STAGES)):
+                if STAGES[stage] <= owners:
+                    low, high = CAP * STAGES[stage - 1], CAP * STAGES[stage]
+                    later = got[stage][jnp.clip(at - low, 0, high - low - 1)]
+                    block = jnp.where(at >= low, later, block)
+            xc[pl.ds((begin + i) * BLK, BLK), :] = block
+
+        def image_step(g, carry, cols=cols, begin=begin, end=end, last=owners == GROUP):
+            rows = [
+                jnp.concatenate([held[index_s[g * PER + i, c]] for c in cols], axis=1)
+                for i in range(PER)
+            ]
+            lhs = jnp.concatenate(rows, axis=0)
+            known = xc[pl.ds(begin * BLK, (end - begin) * BLK), :]
+            image = jnp.dot(lhs, known, preferred_element_type=f32)
+            start = pl.multiple_of(g * (PER * BLK), PER * BLK)
+            if begin > 0:
+                image = image + sums[pl.ds(start, PER * BLK), :]
+            if last:
+                images_t[:, pl.ds(start, PER * BLK)] = image.T.astype(bf16)
+            else:
+                sums[pl.ds(start, PER * BLK), :] = image
+            return carry
+
+        lax.fori_loop(0, RB_DEV // PER, image_step, 0)
+        begin = end
     for c in copies:
-        c.wait()
-
-    for c in range(ntouch):
-        holder = holders[c]
-        xc[pl.ds(c * BLK, BLK), :] = got[holder, slots[c] - CAP * holder]
-
-    def image_step(g, carry):
-        rows = [
-            jnp.concatenate(
-                [held[index_s[g * PER + i, c]] for c in range(ntouch)], axis=1
-            )
-            for i in range(PER)
-        ]
-        lhs = jnp.concatenate(rows, axis=0)
-        image = jnp.dot(lhs, xc[...], preferred_element_type=f32)
-        start = pl.multiple_of(g * (PER * BLK), PER * BLK)
-        images_t[:, pl.ds(start, PER * BLK)] = image.T.astype(bf16)
-        return carry
-
-    lax.fori_loop(0, RB_DEV // PER, image_step, 0)
+        c.wait_send()
 
     def normal_step(g, carry):
         cols = []
         for i in range(2):
-            c = index_s[RB_DEV, 2 * g + i]
+            c = index_s[ORDER, 2 * g + i]
             cols.append(
                 jnp.concatenate([held[index_s[r, c]] for r in range(RB_DEV)], axis=0)
             )
@@ -253,7 +292,7 @@
             done = until
         p = peer_of(me, *OFFSETS[q])
         for k in range(CAP):
-            at = index_s[RB_DEV + 1, CAP * q + k]
+            at = index_s[PLACE, CAP * q + k]
             out[p, k] = codes[at]
             scales[p, pl.ds(k, 1), :] = code_scales[pl.ds(at, 1), :]
         for src, dst, ss, rs in (
@@ -271,7 +310,7 @@
             c.start()
             copies.append(c)
     for k in range(CAP):
-        at = index_s[RB_DEV + 1, CAP * (GROUP - 1) + k]
+        at = index_s[PLACE, CAP * (GROUP - 1) + k]
         arrived[me, k] = codes[at]
         arrived_scales[me, pl.ds(k, 1), :] = code_scales[pl.ds(at, 1), :]
     for c in copies:
@@ -283,8 +322,9 @@
     return high, (value - high.astype(f32)).astype(bf16)
 
 
-def gather_kernel(incoming, arrived, scales, normal):
+def gather_kernel(incoming, arrived, scales, pair, gram, normal, both):
     normal[...] = jnp.zeros_like(normal)
+    both[...] = jnp.zeros_like(both)
 
     def add(s, c):
         row = incoming[s]
@@ -298,24 +338,26 @@
         return c
 
     lax.fori_loop(0, SLOTS, add, 0)
-
-
-def reduce_kernel(
-    voxels, normal, total, held, both, mine, first, part, second, s1, r1, s2, r2, s3, r3, lsem
-):
+    per = normal.shape[0] // CHUNKS
+
+    def accumulate(g, c):
+        high, low = split(normal[pl.ds(g * per, per)].reshape(per * BLK, BLK))
+        value = jnp.concatenate([high, low], axis=1)
+        pair[pl.ds(pl.multiple_of(g * (per * BLK), per * BLK), per * BLK), :] = value
+        both[...] += lax.dot_general(
+            high, value, (((0,), (0,)), ((), ())), preferred_element_type=f32
+        )
+        return c
+
+    lax.fori_loop(0, CHUNKS, accumulate, 0)
+    cross = both[:, BLK:]
+    gram[...] = (both[:, :BLK] + cross + cross.T).reshape(gram.shape)
+
+
+def reduce_kernel(voxels, mine, total, first, part, second, s1, r1, s2, r2, s3, r3):
     me = lax.axis_index("dev")
     grp = lax.axis_index("grp")
     groups = lax.axis_size("grp")
-    blocks = held.shape[0]
-    per = blocks // CHUNKS
-    loads = []
-    for i in range(CHUNKS):
-        c = pltpu.make_async_copy(
-            normal.at[pl.ds(i * per, per)], held.at[pl.ds(i * per, per)], lsem.at[i]
-        )
-        c.start()
-        loads.append(c)
-
     barrier = pltpu.get_barrier_semaphore()
     for dx, dz in OFFSETS:
         pl.semaphore_signal(
@@ -325,23 +367,6 @@
         pl.semaphore_signal(
             barrier, inc=1, device_id={"grp": lax.rem(grp + o, groups)}, device_id_type=MESH
         )
-
-    both[...] = jnp.zeros_like(both)
-    for c in loads:
-        c.wait()
-
-    def accumulate(g, c):
-        rows = held[pl.ds(g * per, per)].reshape(per * BLK, BLK)
-        high, low = split(rows)
-        pair = jnp.concatenate([high, low], axis=1)
-        both[...] += lax.dot_general(
-            high, pair, (((0,), (0,)), ((), ())), preferred_element_type=f32
-        )
-        return c
-
-    lax.fori_loop(0, CHUNKS, accumulate, 0)
-    cross = both[:, BLK:]
-    mine[...] = (both[:, :BLK] + cross + cross.T).reshape(mine.shape)
     pl.semaphore_wait(barrier, GROUP - 1 + groups - 1)
 
     copies = []
@@ -446,26 +471,37 @@
     return jnp.concatenate(r_bands, axis=0), jnp.concatenate(w_bands, axis=0)
 
 
-def basis_kernel(total, normal, basis, r_factor, inverse):
-    @pl.when(pl.program_id(0) == 0)
-    def _():
-        rows = lax.broadcasted_iota(jnp.int32, (BLK, BLK), 0)
-        cols = lax.broadcasted_iota(jnp.int32, (BLK, BLK), 1)
-        gram = total[...].reshape(BLK, BLK)
-        gram = gram + jnp.where(rows == cols, gram_shift, 0.0).astype(f32)
-        r_value, lower_inverse = factor(gram)
-        r_factor[...] = r_value
-        high, low = split(lower_inverse.T)
-        inverse[:BLK, :BLK] = high
-        inverse[BLK:, :BLK] = high
-        inverse[:BLK, BLK:] = low
-        inverse[BLK:, BLK:] = jnp.zeros_like(low)
-
-    high, low = split(normal[...])
-    got = jnp.dot(
-        jnp.concatenate([high, low], axis=1), inverse[...], preferred_element_type=f32
-    )
-    basis[...] = got[:, :BLK] + got[:, BLK:]
+def basis_kernel(total, pair, basis, r_factor, inverse, made, sem):
+    rows = lax.broadcasted_iota(jnp.int32, (BLK, BLK), 0)
+    cols = lax.broadcasted_iota(jnp.int32, (BLK, BLK), 1)
+    gram = total[...].reshape(BLK, BLK)
+    gram = gram + jnp.where(rows == cols, gram_shift, 0.0).astype(f32)
+    r_value, lower_inverse = factor(gram)
+    r_factor[...] = r_value
+    high, low = split(lower_inverse.T)
+    inverse[:BLK, :BLK] = high
+    inverse[BLK:, :BLK] = high
+    inverse[:BLK, BLK:] = low
+    inverse[BLK:, BLK:] = jnp.zeros_like(low)
+    step = made.shape[0] // CHUNKS
+
+    def chunk(i):
+        part = pl.ds(pl.multiple_of(i * step, step), step)
+        return part, pltpu.make_async_copy(made.at[part], basis.at[part], sem.at[i])
+
+    def multiply(i, c):
+        part, copy = chunk(i)
+        value = jnp.dot(pair[part, :], inverse[...], preferred_element_type=f32)
+        made[part, :] = value[:, :BLK] + value[:, BLK:]
+        copy.start()
+        return c
+
+    def finish(i, c):
+        chunk(i)[1].wait()
+        return c
+
+    lax.fori_loop(0, CHUNKS, multiply, 0)
+    lax.fori_loop(0, CHUNKS, finish, 0)
 
 
 def local(tiles, tile_ray, tile_col, touched, home, sketch):
@@ -495,9 +531,13 @@
             VMEM((RB_DEV + 8, BLK), i32),
             SMEM((RB_DEV + 8, BLK), i32),
             SMEM((GROUP,), i32),
+            SMEM((GROUP,), i32),
             VMEM((GROUP, CAP, BLK, BLK), bf16),
-            VMEM((GROUP, CAP, BLK, BLK), bf16),
+            VMEM((CAP * STAGES[0], BLK, BLK), bf16),
+            VMEM((CAP * (STAGES[1] - STAGES[0]), BLK, BLK), bf16),
+            VMEM((CAP * (STAGES[2] - STAGES[1]), BLK, BLK), bf16),
             VMEM((ntouch * BLK, BLK), bf16),
+            VMEM((RB_DEV * BLK, BLK), f32),
             VMEM((BLK, RB_DEV * BLK), bf16),
             VMEM((ntouch, BLK, BLK), jnp.int16),
             VMEM((ntouch, BLK), f32),
@@ -510,24 +550,28 @@
         name="cycle",
     )(touched, home, tile_ray, tile_col, sketch.reshape(block_count, BLK, BLK), tiles)
 
-    normal = pl.pallas_call(
+    rows = block_count * BLK
+    came = (incoming, arrived.reshape(SLOTS, BLK, BLK), arrived_scales)
+    pair, gram = pl.pallas_call(
         gather_kernel,
-        out_shape=jax.ShapeDtypeStruct((block_count, BLK, BLK), f32),
+        out_shape=(
+            jax.ShapeDtypeStruct((rows, 2 * BLK), bf16),
+            jax.ShapeDtypeStruct((GROUP, BLK // GROUP, BLK), f32),
+        ),
         in_specs=[sm(), vm(), vm()],
-        out_specs=vm(),
+        out_specs=(vm(), vm()),
+        scratch_shapes=[VMEM((block_count, BLK, BLK), f32), VMEM((BLK, 2 * BLK), f32)],
+        compiler_params=pltpu.CompilerParams(vmem_limit_bytes=24 << 20),
         name="gather",
-    )(incoming, arrived.reshape(SLOTS, BLK, BLK), arrived_scales)
+    )(*(pltpu.with_memory_space_constraint(v, pltpu.HBM) for v in came))
 
     voxels = float(sketch.shape[0] * groups * GROUP)
     total = pl.pallas_call(
         functools.partial(reduce_kernel, voxels),
         out_shape=jax.ShapeDtypeStruct((GROUP, BLK // GROUP, BLK), f32),
-        in_specs=[hbm()],
+        in_specs=[vm()],
         out_specs=vm(),
         scratch_shapes=[
-            VMEM((block_count, BLK, BLK), f32),
-            VMEM((BLK, 2 * BLK), f32),
-            VMEM((GROUP, BLK // GROUP, BLK), f32),
             VMEM((GROUP, BLK // GROUP, BLK), f32),
             VMEM((BLK // GROUP, BLK), f32),
             VMEM((groups, BLK // GROUP, BLK), f32),
@@ -537,32 +581,29 @@
             dma((groups - 1,)),
             dma((peers,)),
             dma((peers,)),
-            dma((CHUNKS,)),
         ],
-        compiler_params=pltpu.CompilerParams(collective_id=3, has_side_effects=True),
+        compiler_params=pltpu.CompilerParams(
+            collective_id=3, has_side_effects=True, vmem_limit_bytes=8 << 20
+        ),
         name="reduce",
-    )(normal)
-
-    rows = block_count * BLK
-    step = rows // 8
+    )(gram)
+
     basis, r_factor = pl.pallas_call(
         basis_kernel,
-        grid=(8,),
         out_shape=(
             jax.ShapeDtypeStruct((rows, BLK), f32),
             jax.ShapeDtypeStruct((BLK, BLK), f32),
         ),
-        in_specs=[
-            pl.BlockSpec((GROUP, BLK // GROUP, BLK), lambda i: (0, 0, 0)),
-            pl.BlockSpec((step, BLK), lambda i: (i, 0)),
+        in_specs=[vm(), vm()],
+        out_specs=(hbm(), vm()),
+        scratch_shapes=[
+            VMEM((2 * BLK, 2 * BLK), bf16),
+            VMEM((rows, BLK), f32),
+            dma((CHUNKS,)),
         ],
-        out_specs=(
-            pl.BlockSpec((step, BLK), lambda i: (i, 0)),
-            pl.BlockSpec((BLK, BLK), lambda i: (0, 0)),
-        ),
-        scratch_shapes=[VMEM((2 * BLK, 2 * BLK), bf16)],
+        compiler_params=pltpu.CompilerParams(vmem_limit_bytes=24 << 20),
         name="basis",
-    )(total, normal.reshape(rows, BLK))
+    )(total, pair)
     return (basis, r_factor)
 
 

time: 104 us -> 95.8 us (0.921)
  Pallas kernels: 103 us -> 94.7 us
    pallas_call x1, Pallas kernels: 22.1 us -> 16.7 us  [local(): pl.pallas_call(functools.partial(reduce_kernel, voxels), out_shape=jax.Sh...]
    pallas_call x2, Pallas kernels: 15.3 us -> 12.1 us  [the longest x1 7.1 us: local(): pl.pallas_call(basis_kernel, out_shape=(jax.ShapeDtypeStruct((rows, BLK),...]
where the time goes in v4:
time: 95.8 us; the launch traced here: 95.5 us
  Pallas kernels  94.7 us (99%)
    pallas_call x1, Pallas kernels, local(): pl.pallas_call(functools.partial(cycle_kernel, block_count), out_shape=(j...  65.9 us
    pallas_call x1, Pallas kernels, local(): pl.pallas_call(functools.partial(reduce_kernel, voxels), out_shape=jax.Sh...  16.7 us
    pallas_call x1, Pallas kernels, local(): pl.pallas_call(basis_kernel, out_shape=(jax.ShapeDtypeStruct((rows, BLK),...  7.1 us
    pallas_call x1, Pallas kernels, local(): pl.pallas_call(gather_kernel, out_shape=(jax.ShapeDtypeStruct((rows, 2 *...  5.03 us

profile of v4, /device:TPU:1, one launch (start us, length us, event | category | flops | bytes accessed | tf_op | source)
XLA Modules:
  0.0 95.5 jit_solution(10464614288586365776)
XLA Ops:
  0.6 65.9 %cycle.1 = (s16[16,3,128,128]{3,2,1,0:T(8,128)(2,1)}, f32[16,8,128]{2,1,0:T(8,128)}, s32[48]{0:T(128)}) custom-call(s32[24]{0:T(128)} %touched.1, s32[8192]{0:T(1024)} %home.1, s32[512]{0:T(512)} %ray.1, s32[512]{0:T(512)} %col.1, bf16[64,128,128]{2,1,0:T(8,128)(2,1)} %bitcast.2, bf16[512,128,128]{2,1,0:T(8,128)(2,1)} %tiles_in.1), custom_call_target="tpu_custom_call" | custom-call | tf_op jit(solution)/shard_map/cycle/pallas_call | solution.py:516
  66.5 5.0 %gather.1 = (bf16[8192,256]{1,0:T(8,128)(2,1)S(1)}, f32[16,8,128]{2,1,0:T(8,128)S(1)}) custom-call(s32[48]{0:T(128)} %get-tuple-element.7.incoming, s16[48,128,128]{2,1,0:T(8,128)(2,1)} %bitcast.3, f32[16,8,128]{2,1,0:T(8,128)} %get-tuple-element.9.scales), custom_call_target="tpu_custom_call" | custom-call | tf_op jit(solution)/shard_map/gather/pallas_call | solution.py:555
  71.5 16.7 %reduce.1.total = f32[16,8,128]{2,1,0:T(8,128)S(1)} custom-call(f32[16,8,128]{2,1,0:T(8,128)S(1)} %get-tuple-element.10.mine), custom_call_target="tpu_custom_call" | custom-call | tf_op jit(solution)/shard_map/reduce/pallas_call | solution.py:569
  88.3 7.1 %basis.1 = (f32[8192,128]{1,0:T(8,128)}, f32[128,128]{1,0:T(8,128)}) custom-call(f32[16,8,128]{2,1,0:T(8,128)S(1)} %reduce.1.total, bf16[8192,256]{1,0:T(8,128)(2,1)S(1)} %get-tuple-element.11.pair), custom_call_target="tpu_custom_call" | custom-call | tf_op jit(solution)/shard_map/basis/pallas_call | solution.py:591

commit v5 on v4

--- a/solution.py
+++ b/solution.py
@@ -45,6 +45,12 @@
 
 OFFSETS = sorted(
     [(dx, dz) for dx in range(SIDE) for dz in range(SIDE) if (dx, dz) != (0, 0)],
+    key=lambda o: ((min(o[0], SIDE - o[0]) + min(o[1], SIDE - o[1])), o),
+)
+
+
+LEAVING = sorted(
+    [(dx, dz) for dx in range(SIDE) for dz in range(SIDE) if (dx, dz) != (0, 0)],
     key=lambda o: (-(min(o[0], SIDE - o[0]) + min(o[1], SIDE - o[1])), o),
 )
 
@@ -56,10 +62,10 @@
 
 def cycle_kernel(
     block_count,
-    touched,
-    home,
-    ray,
-    col,
+    touched_in,
+    home_in,
+    ray_in,
+    col_in,
     sketch_in,
     tiles_in,
     arrived,
@@ -97,11 +103,24 @@
     ssem,
     lsem,
     isem,
+    touched,
+    home,
+    ray,
+    col,
+    nsem,
+    osem,
 ):
     me = lax.axis_index("dev")
     ntouch = touched.shape[0]
     ntiles = ray.shape[0]
     i32 = jnp.int32
+    numbers = []
+    for i, (src, dst) in enumerate(
+        ((touched_in, touched), (home_in, home), (ray_in, ray), (col_in, col))
+    ):
+        c = pltpu.make_async_copy(src, dst, nsem.at[i])
+        c.start()
+        numbers.append(c)
     whole = pltpu.make_async_copy(sketch_in, sketch, ssem)
     whole.start()
     step = ntiles // CHUNKS
@@ -118,8 +137,9 @@
             barrier, inc=1, device_id={"dev": peer_of(me, dx, dz)}, device_id_type=MESH
         )
 
+    for q, (dx, dz) in enumerate(LEAVING + [(0, 0)]):
+        place_s[dx * SIDE + dz] = q
     for q, (dx, dz) in enumerate(OFFSETS + [(0, 0)]):
-        place_s[dx * SIDE + dz] = q
         back = (SIDE - dx) % SIDE * SIDE + (SIDE - dz) % SIDE
         coming_s[back] = (q + 1) % GROUP
     x, z = lax.div(me, SIDE), lax.rem(me, SIDE)
@@ -127,6 +147,8 @@
     row = lax.broadcasted_iota(i32, (8, BLK), 0)
     wanted = jnp.full((8, BLK), -1, i32)
     holders, keys, arrivals = [], [], []
+    for c in numbers:
+        c.wait()
     for j in range(ntouch):
         stored = home[touched[j]]
         holder = lax.rem(lax.div(stored, block_count), GROUP)
@@ -141,12 +163,12 @@
         keys.append(place_s[far] * CAP + n)
         arrivals.append(coming_s[far] * CAP + n)
         wanted = jnp.where(lane == s, lax.rem(stored, block_count), wanted)
-    ask[...] = wanted
-    asked[me] = wanted
+    ask[...] = wanted[:1]
+    asked[me] = wanted[:1]
 
     pl.semaphore_wait(barrier, GROUP - 1)
     asks = []
-    for i, (dx, dz) in enumerate(OFFSETS):
+    for i, (dx, dz) in enumerate(LEAVING):
         c = pltpu.make_async_remote_copy(
             src_ref=ask,
             dst_ref=asked.at[me],
@@ -290,7 +312,7 @@
         if until > done:
             lax.fori_loop(done, until, normal_step, 0)
             done = until
-        p = peer_of(me, *OFFSETS[q])
+        p = peer_of(me, *LEAVING[q])
         for k in range(CAP):
             at = index_s[PLACE, CAP * q + k]
             out[p, k] = codes[at]
@@ -311,8 +333,11 @@
             copies.append(c)
     for k in range(CAP):
         at = index_s[PLACE, CAP * (GROUP - 1) + k]
-        arrived[me, k] = codes[at]
+        out[me, k] = codes[at]
         arrived_scales[me, pl.ds(k, 1), :] = code_scales[pl.ds(at, 1), :]
+    own = pltpu.make_async_copy(out.at[me], arrived.at[me], osem)
+    own.start()
+    copies.append(own)
     for c in copies:
         c.wait()
 
@@ -322,7 +347,9 @@
     return high, (value - high.astype(f32)).astype(bf16)
 
 
-def gather_kernel(incoming, arrived, scales, pair, gram, normal, both):
+def gather_kernel(incoming, arrived_in, scales, pair, gram, normal, both, arrived, sem):
+    fetch = pltpu.make_async_copy(arrived_in, arrived, sem)
+    fetch.start()
     normal[...] = jnp.zeros_like(normal)
     both[...] = jnp.zeros_like(both)
 
@@ -337,6 +364,7 @@
 
         return c
 
+    fetch.wait()
     lax.fori_loop(0, SLOTS, add, 0)
     per = normal.shape[0] // CHUNKS
 
@@ -370,7 +398,7 @@
     pl.semaphore_wait(barrier, GROUP - 1 + groups - 1)
 
     copies = []
-    for i, (dx, dz) in enumerate(OFFSETS):
+    for i, (dx, dz) in enumerate(LEAVING):
         p = peer_of(me, dx, dz)
         c = pltpu.make_async_remote_copy(
             src_ref=mine.at[p],
@@ -412,7 +440,7 @@
     total[me] = chunk / voxels
 
     copies = []
-    for i, (dx, dz) in enumerate(OFFSETS):
+    for i, (dx, dz) in enumerate(LEAVING):
         p = peer_of(me, dx, dz)
         c = pltpu.make_async_remote_copy(
             src_ref=total.at[me],
@@ -520,14 +548,14 @@
             jax.ShapeDtypeStruct((GROUP, 8, BLK), f32),
             jax.ShapeDtypeStruct((SLOTS,), i32),
         ),
-        in_specs=[sm(), sm(), sm(), sm(), hbm(), hbm()],
-        out_specs=(vm(), vm(), sm()),
+        in_specs=[hbm()] * 6,
+        out_specs=(pl.BlockSpec(memory_space=pltpu.HBM), vm(), sm()),
         scratch_shapes=[
             VMEM((block_count, BLK, BLK), bf16),
             VMEM((ntiles + 1, BLK, BLK), bf16),
-            VMEM((8, BLK), i32),
-            VMEM((GROUP, 8, BLK), i32),
-            SMEM((GROUP, 8, BLK), i32),
+            VMEM((1, BLK), i32),
+            VMEM((GROUP, 1, BLK), i32),
+            SMEM((GROUP, 1, BLK), i32),
             VMEM((RB_DEV + 8, BLK), i32),
             SMEM((RB_DEV + 8, BLK), i32),
             SMEM((GROUP,), i32),
@@ -545,7 +573,9 @@
             VMEM((GROUP, 8, BLK), f32),
         ]
         + [dma((peers,))] * 8
-        + [dma((CHUNKS,)), dma, dma, dma],
+        + [dma((CHUNKS,)), dma, dma, dma]
+        + [SMEM(v.shape, i32) for v in (touched, home, tile_ray, tile_col)]
+        + [dma((4,)), dma],
         compiler_params=pltpu.CompilerParams(collective_id=1, has_side_effects=True),
         name="cycle",
     )(touched, home, tile_ray, tile_col, sketch.reshape(block_count, BLK, BLK), tiles)
@@ -558,9 +588,14 @@
             jax.ShapeDtypeStruct((rows, 2 * BLK), bf16),
             jax.ShapeDtypeStruct((GROUP, BLK // GROUP, BLK), f32),
         ),
-        in_specs=[sm(), vm(), vm()],
+        in_specs=[sm(), hbm(), vm()],
         out_specs=(vm(), vm()),
-        scratch_shapes=[VMEM((block_count, BLK, BLK), f32), VMEM((BLK, 2 * BLK), f32)],
+        scratch_shapes=[
+            VMEM((block_count, BLK, BLK), f32),
+            VMEM((BLK, 2 * BLK), f32),
+            VMEM((SLOTS, BLK, BLK), jnp.int16),
+            dma,
+        ],
         compiler_params=pltpu.CompilerParams(vmem_limit_bytes=24 << 20),
         name="gather",
     )(*(pltpu.with_memory_space_constraint(v, pltpu.HBM) for v in came))

time: 95.8 us -> 89.3 us (0.932)
  Pallas kernels: 94.7 us -> 88.2 us
    pallas_call x1, Pallas kernels: 65.9 us -> 58.4 us  [local(): pl.pallas_call(functools.partial(cycle_kernel, block_count), out_shape=(j...]
where the time goes in v5:
time: 89.3 us; the launch traced here: 89 us
  Pallas kernels  88.2 us (99%)
    pallas_call x1, Pallas kernels, local(): pl.pallas_call(functools.partial(cycle_kernel, block_count), out_shape=(j...  58.4 us
    pallas_call x1, Pallas kernels, local(): pl.pallas_call(functools.partial(reduce_kernel, voxels), out_shape=jax.Sh...  17.1 us
    pallas_call x1, Pallas kernels, local(): pl.pallas_call(basis_kernel, out_shape=(jax.ShapeDtypeStruct((rows, BLK),...  7.11 us
    pallas_call x1, Pallas kernels, local(): pl.pallas_call(gather_kernel, out_shape=(jax.ShapeDtypeStruct((rows, 2 *...  5.59 us

profile of v5, /device:TPU:1, one launch (start us, length us, event | category | flops | bytes accessed | tf_op | source)
XLA Modules:
  0.0 89.0 jit_solution(15330500337920103851)
XLA Ops:
  0.6 58.4 %cycle.1 = (s16[16,3,128,128]{3,2,1,0:T(8,128)(2,1)}, f32[16,8,128]{2,1,0:T(8,128)}, s32[48]{0:T(128)}) custom-call(s32[24]{0:T(128)} %touched_in.1, s32[8192]{0:T(1024)} %home_in.1, s32[512]{0:T(512)} %ray_in.1, s32[512]{0:T(512)} %col_in.1, bf16[64,128,128]{2,1,0:T(8,128)(2,1)} %bitcast.2, bf16[512,128,128]{2,1,0:T(8,128)(2,1)} %tiles_in.1), custom_call_target="tpu_custom_call" | custom-call | tf_op jit(solution)/shard_map/cycle/pallas_call | solution.py:544
  59.0 5.6 %gather.1 = (bf16[8192,256]{1,0:T(8,128)(2,1)S(1)}, f32[16,8,128]{2,1,0:T(8,128)S(1)}) custom-call(s32[48]{0:T(128)} %get-tuple-element.7.incoming, s16[48,128,128]{2,1,0:T(8,128)(2,1)} %bitcast.3, f32[16,8,128]{2,1,0:T(8,128)} %get-tuple-element.9.scales), custom_call_target="tpu_custom_call" | custom-call | tf_op jit(solution)/shard_map/gather/pallas_call | solution.py:585
  64.6 17.1 %reduce.1.total = f32[16,8,128]{2,1,0:T(8,128)S(1)} custom-call(f32[16,8,128]{2,1,0:T(8,128)S(1)} %get-tuple-element.10.mine), custom_call_target="tpu_custom_call" | custom-call | tf_op jit(solution)/shard_map/reduce/pallas_call | solution.py:604
  81.8 7.1 %basis.1 = (f32[8192,128]{1,0:T(8,128)}, f32[128,128]{1,0:T(8,128)}) custom-call(f32[16,8,128]{2,1,0:T(8,128)S(1)} %reduce.1.total, bf16[8192,256]{1,0:T(8,128)(2,1)S(1)} %get-tuple-element.11.pair), custom_call_target="tpu_custom_call" | custom-call | tf_op jit(solution)/shard_map/basis/pallas_call | solution.py:626
